TPU v7x, 512 devices: a whole 4x8x8 slice. The times are simulated.
512 devices in a mesh: lat: 16 (over z, core), lon: 32 (over x, y).
Axes of the slice: x: 4, y: 8, z: 8, core: 2. Of those that a mesh axis runs over, the one named last changes fastest.
Arguments:
- fields: bfloat16 [2, 64, 640, 768], P(None, 'lat', None, 'lon'), may hold values from -6 to 6
- kernel: bfloat16 [5, 64, 3, 3, 64, 64], P(None, 'lat'), may hold values from -0.25 to 0.25
- band_low: int32 [5, 64], replicated, may hold values from -2 to 0
- block_shift: int32 [64, 3], replicated, may hold values from -3 to 3
- mix_weight: bfloat16 [5, 640, 640], P(None, 'lon'), may hold values from -0.109375 to 0.109375
Outputs:
- mixed: bfloat16 [2, 64, 768, 640], P(None, 'lat', 'lon')
All inputs are finite; a program needn't handle non-finite values.
Results may differ from a plain program's by a relative error of at most 0.005.
Values may be sent and summed in bfloat16 or wider, within the bound.
A program may use at most 128 MiB of HBM per device.

v0:
```python
import jax
import jax.numpy as jnp
from jax import lax
from jax.sharding import PartitionSpec as P

BL = 64


def from_behind(block, axis, distance):
    devices = range(lax.axis_size(axis))
    route = [(i - distance, i) for i in devices if i - distance in devices]
    return lax.ppermute(block, axis, route)


def take_row(row_blocks, row_index):
    return jnp.take(row_blocks, row_index, axis=2)


def accumulate(source, weights, low_table, shift_table, first_row, first_slot, window):
    members, count, pieces, cells = source.shape
    nblocks = cells // BL
    taps = weights.shape[2]
    blocks = source.reshape(members, count, pieces, nblocks, BL)
    lane_ids = jnp.arange(nblocks, dtype=jnp.int32)
    index = (lane_ids[None, None, :] + shift_table[:, :, None]) % nblocks
    picked = jax.vmap(take_row, in_axes=(1, 0), out_axes=1)(blocks, index)
    row_ids = jnp.arange(count, dtype=jnp.int32)
    tap_ids = jnp.arange(taps, dtype=jnp.int32)
    slot_ids = jnp.arange(window, dtype=jnp.int32)
    target = (
        first_row
        - first_slot
        + row_ids[None, :, None]
        + low_table[:, :, None]
        + tap_ids[None, None, :]
    )
    select = (target[:, None, :, :] == slot_ids[None, :, None, None]).astype(jnp.float32)
    effective = jnp.einsum("kwrt,krtjpq->kwrjpq", select, weights.astype(jnp.float32)).astype(
        jnp.bfloat16
    )
    return jnp.einsum(
        "ercjbp,kwrjpq->kwecbq", picked, effective, preferred_element_type=jnp.float32
    )


def per_device(fields, kernel, band_low, block_shift, mix_weight):
    local_rows = fields.shape[1]
    pieces = lax.all_to_all(fields, "lon", split_axis=2, concat_axis=3, tiled=True)
    start = lax.axis_index("lat") * local_rows
    low_padded = jnp.pad(band_low, ((0, 0), (2, 2)))
    shift_padded = jnp.pad(block_shift, ((2, 2), (0, 0)))
    low_rows = lax.dynamic_slice_in_dim(low_padded, start + 2, local_rows, 1)
    shift_rows = lax.dynamic_slice_in_dim(shift_padded, start + 2, local_rows, 0)
    partial_value = accumulate(
        pieces, kernel, low_rows, shift_rows, start, start - 2, local_rows + 4
    )
    below = from_behind(partial_value[:, local_rows + 2 :], "lat", 1)
    above = from_behind(partial_value[:, :2], "lat", -1)
    filler = jnp.zeros(
        (partial_value.shape[0], local_rows - 2) + partial_value.shape[2:], jnp.float32
    )
    owned = partial_value[:, 2 : local_rows + 2]
    owned = owned + jnp.concatenate([below, filler], axis=1)
    owned = owned + jnp.concatenate([filler, above], axis=1)
    bases, window, members, channel_part, nblocks, width = owned.shape
    conv = owned.astype(jnp.bfloat16).reshape(bases, window, members, channel_part, nblocks * width)
    conv_pixels = lax.all_to_all(conv, "lon", split_axis=4, concat_axis=3, tiled=True)
    summed = jnp.einsum(
        "klecn,kcd->elnd",
        conv_pixels,
        lax.all_gather(mix_weight, "lon", axis=1, tiled=True),
        preferred_element_type=jnp.float32,
    )
    return jax.nn.gelu(summed, approximate=False).astype(jnp.bfloat16)


def solution(mesh):
    placed = (
        P(None, "lat", None, "lon"),
        P(None, "lat", None, None, None, None),
        P(),
        P(),
        P(None, "lon", None),
    )
    return jax.shard_map(
        per_device,
        mesh=mesh,
        in_specs=placed,
        out_specs=P(None, "lat", "lon", None),
        check_vma=False,
    )
```

profile of v0, /device:TPU:264, one launch (start us, length us, event | category | flops | bytes accessed | tf_op | source)
XLA Modules:
  0.0 241.7 jit_solution(3720481163705671911)
XLA Ops:
  6.5 0.0 copy-start
  6.5 0.0 copy-start.3
  6.5 0.0 copy-start.5
  6.5 0.0 copy-start.4
  6.5 2.6 %copy.39 = bf16[2,4,640,24]{3,1,0,2:T(4,128)(2,1)} copy(bf16[2,4,640,24]{2,3,1,0:T(8,128)(2,1)} %param.5) | data formatting | bytes 491520 | tf_op args[0]
  9.1 4.7 %reshape.71 = bf16[32,2,1920]{2,1,0:T(2,128)(2,1)} reshape(bf16[640,2,4,24]{3,2,1,0:T(4,128)(2,1)} %bitcast.128) | data formatting | bytes 491520
  13.9 10.2 %all-to-all-start = ((bf16[32,2,1920]{2,1,0:T(2,128)(2,1)}), bf16[32,2,1920]{2,1,0:T(2,128)(2,1)S(1)}, u32[]{:S(2)}, u32[]{:S(2)}) async-start(bf16[32,2,1920]{2,1,0:T(2,128)(2,1)} %reshape.71), calls=%async_computation | async-start | bytes 491520 | tf_op jit(solution)/shard_map/all_to_all | solution.py:48
  24.1 0.2 all-gather.2.cloned.1.call-start
  24.3 0.0 copy-done.3
  24.3 0.7 copy.54
  25.0 0.0 all-gather.2.cloned.1.call-update
  25.0 0.0 copy-done.5
  25.0 0.1 pad_dynamic-slice_fusion
  25.1 0.1 copy.38
  25.2 0.0 copy-done.4
  25.2 0.1 dynamic-slice_add_fusion
  25.3 0.1 fusion.28
  25.4 0.1 iota_add_fusion
  25.5 0.1 compare_and_fusion
  25.6 0.1 reshape.59
  25.7 0.0 copy-done
  25.7 5.4 %convert_bitcast_fusion = bf16[5,8,4,3,64,64,1,1]{5,1,4,3,2,0,7,6:T(8,128)(2,1)} fusion(bf16[5,4,3,3,64,64]{5,4,3,2,1,0:T(8,128)(2,1)S(1)} %copy-done, s32[5,4,3]{2,1,0:T(4,128)S(1)} %iota_add_fusion), kind=kOutput, calls=%fused_computation.4 | convolution fusion | flops 13763040 | bytes 5406960 | tf_op jit(solution)/shard_map/kwrt,krtjpq->kwrjpq/dot_general | solution.py:38
  31.1 4.9 %all-to-all-done = bf16[32,2,1920]{2,1,0:T(2,128)(2,1)S(1)} async-done(((bf16[32,2,1920]{2,1,0:T(2,128)(2,1)}), bf16[32,2,1920]{2,1,0:T(2,128)(2,1)S(1)}, u32[]{:S(2)}, u32[]{:S(2)}) %all-to-all-start) | async-done | bytes 245792 | tf_op jit(solution)/shard_map/all_to_all | solution.py:48
  36.0 1.8 reshape.72
  37.8 0.5 copy.93
  38.3 1.2 reshape.57
  39.5 0.5 copy.94
  40.0 18.1 %gather_fusion = bf16[144,2,20,64]{3,1,2,0:T(2,128)(2,1)S(1)} fusion(bf16[4,2,20,12,64]{4,1,3,2,0:T(2,128)(2,1)S(1)} %bitcast.124, s32[144]{0:T(256)S(1)} %reshape.59), kind=kCustom, calls=%fused_computation | custom fusion | bytes 1475712 | tf_op jit(solution)/shard_map/vmap(jit(_take))/gather | solution.py:16
  58.1 1.4 fusion.11
  59.5 7.7 %fusion.6 = f32[5,8,2,20,12,64]{5,3,4,2,1,0:T(8,128)S(1)} fusion(bf16[5,8,4,3,64,64,1,1]{5,1,4,3,2,0,7,6:T(8,128)(2,1)} %convert_bitcast_fusion, bf16[2,4,20,3,12,64,1,1]{5,0,2,4,3,1,7,6:T(2,128)(2,1)S(1)} %fusion.11), kind=kOutput, calls=%fused_computation.10 | convolution fusion | flops 1887436800 | bytes 9584640 | tf_op jit(solution)/shard_map/ercjbp,kwrjpq->kwecbq/dot_general | solution.py:41
  67.2 0.0 copy-start.2
  67.2 0.4 fusion.35
  67.6 4.0 %copy-done.2 = f32[5,8,2,20,12,64]{5,3,4,2,1,0:T(8,128)} copy-done((f32[5,8,2,20,12,64]{5,3,4,2,1,0:T(8,128)}, f32[5,8,2,20,12,64]{5,3,4,2,1,0:T(8,128)S(1)}, u32[]{:S(2)}) %copy-start.2) | copy-done | bytes 4915224
  71.6 1.9 copy.46
  73.5 1.9 collective-permute-start
  75.4 1.9 copy.48
  77.3 4.9 %collective-permute-start.1 = (f32[5,2,2,20,12,64]{5,2,4,3,1,0:T(2,128)S(1)}, f32[5,2,2,20,12,64]{5,2,4,3,1,0:T(2,128)S(1)}, u32[]{:S(2)}, u32[]{:S(2)}) collective-permute-start(f32[5,2,2,20,12,64]{5,2,4,3,1,0:T(2,128)S(1)} %copy.48), channel_id=1, source_target_pairs={{32,0},{64,32},{96,64},{128,96},{160,128},{192,160},{224,192},{256... | collective-permute-start | bytes 3686408 | tf_op jit(solution)/shard_map/ppermute | solution.py:12
  82.2 23.7 %collective-permute-done = f32[5,2,2,20,12,64]{5,2,4,3,1,0:T(2,128)S(1)} collective-permute-done((f32[5,2,2,20,12,64]{5,2,4,3,1,0:T(2,128)S(1)}, f32[5,2,2,20,12,64]{5,2,4,3,1,0:T(2,128)S(1)}, u32[]{:S(2)}, u32[]{:S(2)}) %collective-permute-start) | collective-permute-done | bytes 1228832 | tf_op jit(solution)/shard_map/ppermute | solution.py:12
  105.9 0.5 copy.47
  106.4 3.2 %collective-permute-done.1 = f32[5,2,2,20,12,64]{5,2,4,3,1,0:T(2,128)S(1)} collective-permute-done((f32[5,2,2,20,12,64]{5,2,4,3,1,0:T(2,128)S(1)}, f32[5,2,2,20,12,64]{5,2,4,3,1,0:T(2,128)S(1)}, u32[]{:S(2)}, u32[]{:S(2)}) %collective-permute-start.1) | collective-permute-done | bytes 1228832 | tf_op jit(solution)/shard_map/ppermute | solution.py:12
  109.5 0.5 copy.49
  110.0 5.5 %fusion.3 = bf16[5,4,2,20,12,64]{5,3,4,2,1,0:T(8,128)(2,1)} fusion(f32[5,8,2,20,12,64]{5,3,4,2,1,0:T(8,128)} %copy-done.2, f32[5,2,2,20,12,64]{5,3,4,2,1,0:T(8,128)S(1)} %copy.49, f32[5,2,2,20,12,64]{5,3,4,2,1,0:T(8,128)S(1)} %copy.47), kind=kLoop, calls=%fused_computation.7 | loop fusion | flops 1843200 | bytes 6144000 | tf_op jit(solution)/shard_map/convert_element_type | solution.py:66
  115.6 10.8 %copy.70 = bf16[5,4,2,20,12,64]{3,1,2,0,5,4:T(4,128)(2,1)} copy(bf16[5,4,2,20,12,64]{5,3,4,2,1,0:T(8,128)(2,1)} %fusion.3) | data formatting | bytes 2457600 | tf_op jit(solution)/shard_map/reshape | solution.py:66
  126.3 15.9 %reshape.73 = bf16[32,2,9600]{2,1,0:T(2,128)(2,1)S(1)} reshape(bf16[768,5,2,4,20]{4,3,2,1,0:T(4,128)(2,1)} %bitcast.121) | data formatting | bytes 2457600
  142.2 38.9 %all_to_all.33 = bf16[32,2,9600]{2,1,0:T(2,128)(2,1)S(1)} all-to-all(bf16[32,2,9600]{2,1,0:T(2,128)(2,1)S(1)} %reshape.73), channel_id=1, replica_groups=mesh['lat'=16,'lon'=32] {'lon'}, dimensions={0} | all-to-all | bytes 2457600 | tf_op jit(solution)/shard_map/all_to_all | solution.py:67
  181.1 20.8 %reshape.74 = bf16[768,5,2,4,20]{4,3,2,1,0:T(4,128)(2,1)} reshape(bf16[32,2,9600]{2,1,0:T(2,128)(2,1)S(1)} %all_to_all.33) | data formatting | bytes 2457600
  201.9 11.3 %copy.92 = bf16[5,4,2,20,32,24]{3,4,5,2,1,0:T(8,128)(2,1)} copy(bf16[5,4,2,20,32,24]{3,1,2,0,5,4:T(4,128)(2,1)} %bitcast.122) | data formatting | bytes 2457600 | tf_op jit(solution)/shard_map/all_to_all | solution.py:67
  213.2 14.7 %all_to_all.30 = bf16[5,4,2,640,24]{3,4,2,1,0:T(8,128)(2,1)} reshape(bf16[5,4,2,32,20,24]{4,3,5,2,1,0:T(8,128)(2,1)} %bitcast.123) | data formatting | bytes 2457600 | tf_op jit(solution)/shard_map/all_to_all | solution.py:67
  227.9 0.0 all-gather.2.cloned.1.call-done
  227.9 0.0 copy-start.1
  228.0 4.9 %fusion.4 = f32[4,2,24,640,1]{3,2,0,1,4:T(8,128)S(1)} fusion(bf16[5,640,640,1,1]{2,0,1,4,3:T(8,128)(2,1)} %bitcast.129, bf16[5,4,2,640,24]{3,4,2,1,0:T(8,128)(2,1)} %all_to_all.30), kind=kOutput, calls=%fused_computation.8 | convolution fusion | flops 786432000 | bytes 5816320 | tf_op jit(solution)/shard_map/klecn,kcd->elnd/dot_general | solution.py:68
  232.8 1.1 fusion.15
  233.9 0.7 copy.56
  234.6 0.0 copy-done.1
  (1 shorter events, 0.0 us)
Async XLA Ops:
  6.5 19.1 %copy-start = (bf16[5,4,3,3,64,64]{5,4,3,2,1,0:T(8,128)(2,1)S(1)}, bf16[5,4,3,3,64,64]{5,4,3,2,1,0:T(8,128)(2,1)}, u32[]{:S(2)}) copy-start(bf16[5,4,3,3,64,64]{5,4,3,2,1,0:T(8,128)(2,1)} %param.6) | copy-start | bytes 4423684
  6.5 17.7 %copy-start.3 = (bf16[5,20,640]{2,1,0:T(8,128)(2,1)S(1)}, bf16[5,20,640]{2,1,0:T(8,128)(2,1)}, u32[]{:S(2)}) copy-start(bf16[5,20,640]{2,1,0:T(8,128)(2,1)} %param.9) | copy-start | bytes 384004
  6.5 18.5 %copy-start.5 = (s32[64,3]{0,1:T(4,128)S(1)}, s32[64,3]{0,1:T(4,128)}, u32[]{:S(2)}) copy-start(s32[64,3]{0,1:T(4,128)} %param.8) | copy-start | bytes 2308
  6.5 18.7 %copy-start.4 = (s32[5,64]{1,0:T(8,128)S(1)}, s32[5,64]{1,0:T(8,128)}, u32[]{:S(2)}) copy-start(s32[5,64]{1,0:T(8,128)} %param.7) | copy-start | bytes 3844
  13.9 22.1 %all-to-all-start = ((bf16[32,2,1920]{2,1,0:T(2,128)(2,1)}), bf16[32,2,1920]{2,1,0:T(2,128)(2,1)S(1)}, u32[]{:S(2)}, u32[]{:S(2)}) async-start(bf16[32,2,1920]{2,1,0:T(2,128)(2,1)} %reshape.71), calls=%async_computation | async-start | bytes 491520 | tf_op jit(solution)/shard_map/all_to_all | solution.py:48
  24.1 203.9 %all-gather.2.cloned.1.call-start = ((), (), s32[]{:S(2)}) async-start(), calls=%async_computation.2 | async-start | bytes 6758400 | tf_op jit(solution)/shard_map/all_gather | solution.py:71
  67.2 4.4 %copy-start.2 = (f32[5,8,2,20,12,64]{5,3,4,2,1,0:T(8,128)}, f32[5,8,2,20,12,64]{5,3,4,2,1,0:T(8,128)S(1)}, u32[]{:S(2)}) copy-start(f32[5,8,2,20,12,64]{5,3,4,2,1,0:T(8,128)S(1)} %fusion.6) | copy-start | bytes 14745604
  73.5 32.4 %collective-permute-start = (f32[5,2,2,20,12,64]{5,2,4,3,1,0:T(2,128)S(1)}, f32[5,2,2,20,12,64]{5,2,4,3,1,0:T(2,128)S(1)}, u32[]{:S(2)}, u32[]{:S(2)}) collective-permute-start(f32[5,2,2,20,12,64]{5,2,4,3,1,0:T(2,128)S(1)} %copy.46), channel_id=1, source_target_pairs={{0,32},{32,64},{64,96},{96,128},{128,160},{160,192},{192,224},{224... | collective-permute-start | bytes 3686408 | tf_op jit(solution)/shard_map/ppermute | solution.py:12
  77.3 32.3 %collective-permute-start.1 = (f32[5,2,2,20,12,64]{5,2,4,3,1,0:T(2,128)S(1)}, f32[5,2,2,20,12,64]{5,2,4,3,1,0:T(2,128)S(1)}, u32[]{:S(2)}, u32[]{:S(2)}) collective-permute-start(f32[5,2,2,20,12,64]{5,2,4,3,1,0:T(2,128)S(1)} %copy.48), channel_id=1, source_target_pairs={{32,0},{64,32},{96,64},{128,96},{160,128},{192,160},{224,192},{256... | collective-permute-start | bytes 3686408 | tf_op jit(solution)/shard_map/ppermute | solution.py:12
  227.9 6.7 %copy-start.1 = (bf16[5,4,3,3,64,64]{5,4,3,2,1,0:T(8,128)(2,1)S(1)}, bf16[5,4,3,3,64,64]{5,4,3,2,1,0:T(8,128)(2,1)}, u32[]{:S(2)}) copy-start(bf16[5,4,3,3,64,64]{5,4,3,2,1,0:T(8,128)(2,1)} %param.6) | copy-start | bytes 4423684
Sparse Core Ops, SparseCore 0:
  28.0 95.8 all-gather.1
where the time goes:
time: 246 us; the launch traced here: 242 us
  local copies, waits for them, and re-layouts  114 us (46%)
  blocking collectives  38.9 us (16%)
  waiting for transfers between devices  31.9 us (13%)
  matrix products  18 us (7%)
  starting transfers between devices  17.2 us (7%)
  between operations  13.8 us (6%)
  other arithmetic  8.32 us (3%)
    unnamed x18, local copies, waits for them, and re-layouts  50.5 us
    all_to_all x1, blocking collectives, per_device(): lax.all_to_all(conv, 'lon', split_axis=4, concat_axis=3, tiled=True)  38.9 us
    ppermute x2, waiting for transfers between devices, from_behind(): return lax.ppermute(block, axis, route)  26.9 us
    all_to_all x2, local copies, waits for them, and re-layouts, per_device(): lax.all_to_all(conv, 'lon', split_axis=4, concat_axis=3, tiled=True)  26.1 us
    gather x2, local copies, waits for them, and re-layouts, take_row(): return jnp.take(row_blocks, row_index, axis=2)  18.2 us
    reshape x1, local copies, waits for them, and re-layouts, per_device(): owned.astype(jnp.bfloat16)  10.8 us
    all_to_all x1, starting transfers between devices, per_device(): lax.all_to_all(fields, 'lon', split_axis=2, concat_axis=3, tiled=True)  10.2 us
    dot_general x1, matrix products, accumulate(): jnp.einsum('ercjbp,kwrjpq->kwecbq', picked, effective, preferred_element_...  7.67 us
  transfers between devices with their start and end apart: 4, of which 3 were waited for; matrix products, arithmetic and copies ran while one was open for 44% of the time, Pallas kernels for 0%

commit v1 on v0

v1 whole, which is shorter than its diff:
```python
import jax
import jax.numpy as jnp
from jax import lax
from jax.experimental import pallas as pl
from jax.experimental.pallas import tpu as pltpu
from jax.sharding import PartitionSpec as P

MESH = pl.DeviceIdType.MESH
F32 = jnp.float32
BF16 = jnp.bfloat16
NLAT, NLON = 16, 32


def pack_kernel(f_ref, w_ref, m_ref, wp_ref):
    rows = [f_ref[:, r].astype(F32).reshape(48, 640) for r in range(4)]
    gap = jnp.zeros((48, 48), F32)
    for g in range(16):
        cut = [row[:, 40 * g : 40 * g + 40] for row in rows]
        packed = jnp.concatenate([cut[0], cut[1], gap, cut[2], cut[3], gap], axis=1)
        m_ref[g] = packed.reshape(2, 24, 256).astype(BF16)
    odd = lax.rem(lax.axis_index("lon"), 2) == 1
    four = jnp.zeros((4, 640), F32)
    for k in range(5):
        w = w_ref[k].astype(F32)
        padded = jnp.where(
            odd,
            jnp.concatenate([four, w], axis=0),
            jnp.concatenate([w, four], axis=0),
        )
        wp_ref[3 * k : 3 * k + 3] = padded.reshape(3, 8, 640).astype(BF16)
    wp_ref[15] = jnp.zeros((8, 640), BF16)


def remote(src, dst, send, recv, where):
    return pltpu.make_async_remote_copy(
        src_ref=src,
        dst_ref=dst,
        send_sem=send,
        recv_sem=recv,
        device_id=where,
        device_id_type=MESH,
    )


def spread_kernel(
    m_ref, wp_ref, k_ref, r_ref, kh_ref, g_ref,
    m_send, m_recv, w_send, w_recv, h_send, h_recv, k_send, k_recv, own_sem,
):
    lat = lax.axis_index("lat")
    lon = lax.axis_index("lon")
    up = lax.rem(lat + 1, NLAT)
    down = lax.rem(lat + NLAT - 1, NLAT)
    barrier = pltpu.get_barrier_semaphore()

    def greet(j, c):
        pl.semaphore_signal(
            barrier, inc=1, device_id={"lon": lax.rem(lon + j, NLON)}, device_id_type=MESH
        )
        return c

    lax.fori_loop(1, NLON, greet, 0)
    pl.semaphore_signal(barrier, inc=1, device_id={"lat": up}, device_id_type=MESH)
    pl.semaphore_signal(barrier, inc=1, device_id={"lat": down}, device_id_type=MESH)
    pl.semaphore_wait(barrier, NLON + 1)

    own_m = pltpu.make_async_copy(m_ref.at[lon], r_ref.at[1, lon], own_sem.at[0])
    own_w = pltpu.make_async_copy(wp_ref.at[lat], g_ref.at[lon], own_sem.at[1])
    own_m.start()
    own_w.start()

    def send_m(j):
        to = lax.rem(lon + j, NLON)
        return remote(
            m_ref.at[to], r_ref.at[1, lon], m_send.at[to], m_recv.at[lon], {"lon": to}
        )

    def send_w(j):
        to = lax.rem(lon + j, NLON)
        return remote(
            wp_ref.at[lat], g_ref.at[lon], w_send.at[to], w_recv.at[lon], {"lon": to}
        )

    def start_m(j, c):
        send_m(j).start()
        return c

    def start_w(j, c):
        send_w(j).start()
        return c

    lax.fori_loop(1, NLON, start_m, 0)
    k_down = remote(
        k_ref.at[:, pl.ds(0, 2)], kh_ref.at[1], k_send.at[0], k_recv.at[0], {"lat": down}
    )
    k_up = remote(
        k_ref.at[:, pl.ds(2, 2)], kh_ref.at[0], k_send.at[1], k_recv.at[1], {"lat": up}
    )
    k_down.start()
    k_up.start()
    lax.fori_loop(1, NLON, start_w, 0)

    def take_m(j, c):
        src = lax.rem(lon + NLON - j, NLON)
        remote(
            m_ref.at[lon], r_ref.at[1, src], m_send.at[src], m_recv.at[src], {"lon": src}
        ).wait_recv()
        return c

    own_m.wait()
    lax.fori_loop(1, NLON, take_m, 0)
    h_down = remote(
        r_ref.at[1, :, :, pl.ds(0, 128)], r_ref.at[2, :, :, pl.ds(0, 128)],
        h_send.at[0], h_recv.at[0], {"lat": down},
    )
    h_up = remote(
        r_ref.at[1, :, :, pl.ds(128, 128)], r_ref.at[0, :, :, pl.ds(128, 128)],
        h_send.at[1], h_recv.at[1], {"lat": up},
    )
    h_down.start()
    h_up.start()

    def take_w(j, c):
        src = lax.rem(lon + NLON - j, NLON)
        remote(
            wp_ref.at[lat], g_ref.at[src], w_send.at[src], w_recv.at[src], {"lon": src}
        ).wait_recv()
        return c

    own_w.wait()
    lax.fori_loop(1, NLON, take_w, 0)

    def sent(j, c):
        send_m(j).wait_send()
        send_w(j).wait_send()
        return c

    lax.fori_loop(1, NLON, sent, 0)
    k_down.wait()
    k_up.wait()
    h_down.wait()
    h_up.wait()


ROWS = ((0, 2), (0, 3), (1, 0), (1, 1), (1, 2), (1, 3), (2, 0), (2, 1))


def conv_kernel(
    low_ref, shift_ref, r_ref, k_ref, kh_ref, a_ref, x_ref, lhs_ref, rhs_ref, acc_ref, sp_ref
):
    lat = lax.axis_index("lat")
    first = 4 * lat - 2
    half = lax.broadcasted_iota(jnp.int32, (80, 128), 1) < 64

    q = lax.broadcasted_iota(jnp.int32, (64, 256), 0)
    lane = lax.broadcasted_iota(jnp.int32, (64, 256), 1)
    base = 32 * (q >> 3) + (q & 7)
    for o in range(4):
        sp_ref[o] = jnp.where(lane == base + 8 * o, 1.0, 0.0).astype(BF16)
    sp_ref[4] = jnp.zeros((64, 256), BF16)

    for s, pairs in ((0, (1,)), (1, (0, 1)), (2, (0,))):
        for h in pairs:

            def turn(p, c, s=s, h=h):
                rows = pl.ds(pl.multiple_of(128 * p, 128), 128)
                t = r_ref[s, rows, 128 * h : 128 * h + 128].astype(F32).T[0:80]
                u = pltpu.roll(t, 64, 1)
                x_ref[s, 2 * p, 80 * h : 80 * h + 80] = jnp.where(half, t, u)
                x_ref[s, 2 * p + 1, 80 * h : 80 * h + 80] = jnp.where(half, u, t)
                return c

            lax.fori_loop(0, 6, turn, 0)

    left = lax.broadcasted_iota(jnp.int32, (40, 128), 1) < 64
    for i, (s, r) in enumerate(ROWS):
        row = jnp.clip(first + i, 0, 63)
        shifts = [shift_ref[row, j] for j in range(3)]

        def gather(p, c, i=i, s=s, r=r, shifts=shifts):
            out = []
            for b in range(2):
                blocks = [lax.rem(2 * p + b + sh + 12, 12) for sh in shifts]
                x0, x1, x2 = [x_ref[s, n, 40 * r : 40 * r + 40] for n in blocks]
                out.append(jnp.concatenate([jnp.where(left, x0, x1), x2], axis=1))
            rows = pl.ds(pl.multiple_of(80 * p, 16), 80)
            lhs_ref[rows, 256 * i : 256 * i + 256] = jnp.concatenate(out, axis=0).astype(BF16)
            return c

        lax.fori_loop(0, 6, gather, 0)
        rhs_ref[256 * i + 192 : 256 * i + 256] = jnp.zeros((64, 256), BF16)

    def basis(k, c):
        for i, (s, r) in enumerate(ROWS):
            row = first + i
            low = low_ref[k, jnp.clip(row, 0, 63)]
            total = jnp.zeros((192, 256), F32)
            for t in range(3):
                o = i - 2 + low + t
                good = (o >= 0) & (o < 4) & (row >= 0) & (row < 64)
                slot = jnp.where(good, o, 4)
                if s == 1:
                    weights = k_ref[k, r, t]
                else:
                    weights = kh_ref[s // 2, k, r % 2, t]
                total = total + jnp.dot(
                    weights.reshape(192, 64), sp_ref[slot], preferred_element_type=F32
                )
            rhs_ref[256 * i : 256 * i + 192] = total.astype(BF16)
        acc_ref[k] = jnp.dot(lhs_ref[...], rhs_ref[...], preferred_element_type=F32)
        return c

    lax.fori_loop(0, 5, basis, 0)

    tail = jnp.zeros((40, 32), F32)
    for y in range(8):
        groups = [divmod(3 * y + n, 8) for n in range(3)]
        for x in range(4):
            parts = []
            for k in range(5):
                n = 0
                while n < 3:
                    beta, qg = groups[n]
                    m = n
                    while m < 3 and groups[m][0] == beta:
                        m += 1
                    rows = slice(40 * (3 * x + beta), 40 * (3 * x + beta) + 40)
                    parts.append(acc_ref[k, rows, 32 * qg : 32 * (qg + m - n)])
                    n = m
            a_ref[x, y] = jnp.concatenate(parts + [tail], axis=1).astype(BF16)


def return_kernel(
    a_ref, g_ref, ra_ref, ga_ref, a_send, a_recv, c_send, c_recv, s_send, s_recv, own_sem
):
    lat = lax.axis_index("lat")
    lon = lax.axis_index("lon")
    up = lax.rem(lat + 2, NLAT)
    down = lax.rem(lat + NLAT - 2, NLAT)
    twin = lat + 1 - 2 * lax.rem(lat, 2)
    barrier = pltpu.get_barrier_semaphore()

    def greet(j, c):
        pl.semaphore_signal(
            barrier, inc=1, device_id={"lon": lax.rem(lon + j, NLON)}, device_id_type=MESH
        )
        return c

    lax.fori_loop(1, NLON, greet, 0)
    for other in (up, down, twin):
        pl.semaphore_signal(barrier, inc=1, device_id={"lat": other}, device_id_type=MESH)
    pl.semaphore_wait(barrier, NLON + 2)

    def piece_up(n, base):
        return lax.rem(base + 2 * NLAT - 2 * n, NLAT)

    def piece_down(n, base):
        return lax.rem(base + 2 * n, NLAT)

    started = []

    def go(copy):
        copy.start()
        started.append(copy)

    def ring_up(n):
        src = g_ref if n == 0 else ga_ref.at[piece_up(n, lat)]
        return remote(
            src, ga_ref.at[piece_up(n, lat)], c_send.at[n], c_recv.at[n], {"lat": up}
        )

    def ring_down(n):
        src = g_ref if n == 0 else ga_ref.at[piece_down(n, lat)]
        return remote(
            src, ga_ref.at[piece_down(n, lat)], c_send.at[4 + n], c_recv.at[4 + n], {"lat": down}
        )

    def to_twin(slot, piece, src):
        return remote(
            src, ga_ref.at[piece], s_send.at[slot], s_recv.at[slot], {"lat": twin}
        )

    go(ring_up(0))
    go(ring_down(0))

    def send_a(j):
        to = lax.rem(lon + j, NLON)
        return remote(
            a_ref.at[to], ra_ref.at[lon], a_send.at[to], a_recv.at[lon], {"lon": to}
        )

    def start_a(j, c):
        send_a(j).start()
        return c

    lax.fori_loop(1, NLON, start_a, 0)
    own_a = pltpu.make_async_copy(a_ref.at[lon], ra_ref.at[lon], own_sem.at[0])
    own_g = pltpu.make_async_copy(g_ref, ga_ref.at[lat], own_sem.at[1])
    own_a.start()
    own_g.start()
    go(to_twin(0, lat, g_ref))

    for n in range(1, 5):
        piece = piece_up(n, lat)
        remote(
            g_ref, ga_ref.at[piece], c_send.at[n - 1], c_recv.at[n - 1], {"lat": up}
        ).wait_recv()
        if n < 4:
            go(ring_up(n))
        go(to_twin(n, piece, ga_ref.at[piece]))
        if n < 4:
            piece = piece_down(n, lat)
            remote(
                g_ref, ga_ref.at[piece], c_send.at[3 + n], c_recv.at[3 + n], {"lat": down}
            ).wait_recv()
            if n < 3:
                go(ring_down(n))
            go(to_twin(4 + n, piece, ga_ref.at[piece]))

    def take_a(j, c):
        src = lax.rem(lon + NLON - j, NLON)
        remote(
            a_ref.at[lon], ra_ref.at[src], a_send.at[src], a_recv.at[src], {"lon": src}
        ).wait_recv()
        send_a(j).wait_send()
        return c

    lax.fori_loop(1, NLON, take_a, 0)
    for slot in range(8):
        piece = piece_up(slot, twin) if slot < 5 else piece_down(slot - 4, twin)
        remote(
            g_ref, ga_ref.at[piece], s_send.at[slot], s_recv.at[slot], {"lat": twin}
        ).wait_recv()
    for copy in started:
        copy.wait_send()
    own_a.wait()
    own_g.wait()


def mix_kernel(ra_ref, g_ref, o_ref, t_ref, acc_ref):
    k = pl.program_id(0)

    @pl.when(k == 0)
    def _():
        for e in range(2):
            a = ra_ref[:, e].astype(F32).reshape(640, 512)
            t_ref[e] = a.T.astype(BF16)
        acc_ref[...] = jnp.zeros_like(acc_ref)

    def part(r, h):
        return g_ref[r, :, h].astype(F32)

    w = jnp.stack(
        [part(0, 0), part(1, 0), part(2, 0) + part(0, 1), part(1, 1), part(2, 1)], axis=1
    )
    w = w.reshape(640, 640).astype(BF16)
    rows = pl.ds(pl.multiple_of(96 * k, 32), 96)
    for e in range(2):
        acc_ref[e] += jnp.dot(t_ref[e, rows], w, preferred_element_type=F32)

    @pl.when(k == 4)
    def _():
        for e in range(2):
            v = acc_ref[e].reshape(3, 4, 8, 640)
            v = v * (1.0 + lax.erf(v * 0.7071067811865476)) * 0.5
            for o in range(4):
                o_ref[e, o] = v[:, o].reshape(24, 640).astype(BF16)


def per_device(fields, kernel, band_low, block_shift, mix_weight):
    whole = pl.BlockSpec(memory_space=pltpu.VMEM)
    smem = pl.BlockSpec(memory_space=pltpu.SMEM)
    anywhere = pl.BlockSpec(memory_space=pl.ANY)
    shape = jax.ShapeDtypeStruct
    dma = pltpu.SemaphoreType.DMA

    cells_first = jnp.transpose(fields, (0, 1, 3, 2))
    messages, pieces = pl.pallas_call(
        pack_kernel,
        out_shape=(shape((16, 2, 24, 256), BF16), shape((16, 8, 640), BF16)),
        in_specs=[whole, whole],
        out_specs=(whole, whole),
        name="pack",
    )(cells_first, mix_weight)
    received, kernel_halo, gathered = pl.pallas_call(
        spread_kernel,
        out_shape=(
            shape((3, 32, 24, 256), BF16),
            shape((2, 5, 2, 3, 3, 64, 64), BF16),
            shape((32, 8, 640), BF16),
        ),
        in_specs=[anywhere] * 3,
        out_specs=(anywhere,) * 3,
        scratch_shapes=[
            dma((32,)), dma((32,)), dma((32,)), dma((32,)),
            dma((2,)), dma((2,)), dma((2,)), dma((2,)), dma((2,)),
        ],
        compiler_params=pltpu.CompilerParams(collective_id=0, has_side_effects=True),
        name="spread",
    )(messages.reshape(32, 24, 256), pieces, kernel)
    convolved = pl.pallas_call(
        conv_kernel,
        out_shape=shape((4, 8, 40, 512), BF16),
        in_specs=[smem, smem, whole, whole, whole],
        out_specs=whole,
        scratch_shapes=[
            pltpu.VMEM((3, 12, 160, 128), F32),
            pltpu.VMEM((480, 2048), BF16),
            pltpu.VMEM((2048, 256), BF16),
            pltpu.VMEM((5, 480, 256), F32),
            pltpu.VMEM((5, 64, 256), BF16),
        ],
        name="conv",
    )(band_low, block_shift, received.reshape(3, 768, 256), kernel, kernel_halo)
    returned, weights = pl.pallas_call(
        return_kernel,
        out_shape=(shape((32, 40, 512), BF16), shape((16, 32, 8, 640), BF16)),
        in_specs=[anywhere] * 2,
        out_specs=(anywhere,) * 2,
        scratch_shapes=[
            dma((32,)), dma((32,)), dma((7,)), dma((7,)), dma((8,)), dma((8,)), dma((2,)),
        ],
        compiler_params=pltpu.CompilerParams(collective_id=1, has_side_effects=True),
        name="give_back",
    )(convolved.reshape(32, 40, 512), gathered)
    return pl.pallas_call(
        mix_kernel,
        out_shape=shape((2, 4, 24, 640), BF16),
        grid=(5,),
        in_specs=[
            pl.BlockSpec((16, 2, 40, 512), lambda k: (0, 0, 0, 0)),
            pl.BlockSpec((3, 16, 2, 8, 640), lambda k: (k, 0, 0, 0, 0)),
        ],
        out_specs=pl.BlockSpec((2, 4, 24, 640), lambda k: (0, 0, 0, 0)),
        scratch_shapes=[pltpu.VMEM((2, 512, 640), BF16), pltpu.VMEM((2, 96, 640), F32)],
        name="mix",
    )(returned.reshape(16, 2, 40, 512), weights.reshape(16, 16, 2, 8, 640))


def solution(mesh):
    placed = (
        P(None, "lat", None, "lon"),
        P(None, "lat", None, None, None, None),
        P(),
        P(),
        P(None, "lon", None),
    )
    return jax.shard_map(
        per_device,
        mesh=mesh,
        in_specs=placed,
        out_specs=P(None, "lat", "lon", None),
        check_vma=False,
    )
```

time: 246 us -> 106 us (0.43)
  the two profiles are of different devices: /device:TPU:264 before, /device:TPU:23 now
where the time goes in v1:
time: 106 us
  Pallas kernels  105 us (99%)
  local copies, waits for them, and re-layouts  1.38 us (1%)
    pallas_call x1, Pallas kernels, per_device(): pl.pallas_call(return_kernel, out_shape=(shape((32, 40, 512), BF16), shap...  49.9 us
    pallas_call x1, Pallas kernels, per_device(): pl.pallas_call(spread_kernel, out_shape=(shape((3, 32, 24, 256), BF16), s...  29.6 us
    pallas_call x1, Pallas kernels, per_device(): pl.pallas_call(conv_kernel, out_shape=shape((4, 8, 40, 512), BF16), in_sp...  16.3 us
    pallas_call x1, Pallas kernels, per_device(): pl.pallas_call(mix_kernel, out_shape=shape((2, 4, 24, 640), BF16), grid=(...  6.62 us
    pallas_call x1, Pallas kernels, per_device(): pl.pallas_call(pack_kernel, out_shape=(shape((16, 2, 24, 256), BF16), sha...  2.14 us

profile of v1, /device:TPU:23, one launch (start us, length us, event | category | flops | bytes accessed | tf_op | source)
XLA Modules:
  0.0 106.0 jit_solution(11801037816833789242)
XLA Ops:
  0.0 1.4 %copy.6.shift_ref = s32[64,3]{1,0:T(8,128)} copy(s32[64,3]{0,1:T(4,128)} %param.8) | data formatting | bytes 1536 | tf_op args[3]
  1.4 2.1 %pack.1 = (bf16[16,2,24,256]{3,2,1,0:T(8,128)(2,1)}, bf16[16,8,640]{2,1,0:T(8,128)(2,1)}) custom-call(bf16[2,4,24,640]{3,2,1,0:T(8,128)(2,1)} %bitcast.11, bf16[5,20,640]{2,1,0:T(8,128)(2,1)} %w_ref.1), custom_call_target="tpu_custom_call" | custom-call | tf_op jit(solution)/shard_map/pack/pallas_call | solution.py:377
  3.5 29.6 %spread.1 = (bf16[3,32,24,256]{3,2,1,0:T(8,128)(2,1)}, bf16[2,5,2,3,3,64,64]{6,5,4,3,2,1,0:T(8,128)(2,1)}, bf16[32,8,640]{2,1,0:T(8,128)(2,1)}) custom-call(bf16[32,24,256]{2,1,0:T(8,128)(2,1)} %bitcast.10, bf16[16,8,640]{2,1,0:T(8,128)(2,1)} %get-tuple-element.13.wp_ref, bf16[5,4,3,3,64,64]{5,4,3,2,1,0:T(8,128)(2,1)} %k_ref.3), custom_call_target="tpu_custom_call" | custom-call | tf_op jit(solution)/shard_map/spread/pallas_call | solution.py:384
  33.2 16.3 %conv.1 = bf16[4,8,40,512]{3,2,1,0:T(8,128)(2,1)} custom-call(s32[5,64]{1,0:T(8,128)} %low_ref.1, s32[64,3]{1,0:T(8,128)} %copy.6.shift_ref, bf16[3,768,256]{2,1,0:T(8,128)(2,1)} %bitcast.9, bf16[5,4,3,3,64,64]{5,4,3,2,1,0:T(8,128)(2,1)} %k_ref.3, bf16[2,5,2,3,3,64,64]{6,5,4,3,2,1,0:T(8,128)(2,1)} %get-tuple-element.15.kh_ref), custom_call_target="tpu_custom_call" | custom-call | tf_op jit(solution)/shard_map/conv/pallas_call | solution.py:400
  49.4 49.9 %give_back.1 = (bf16[32,40,512]{2,1,0:T(8,128)(2,1)}, bf16[16,32,8,640]{3,2,1,0:T(8,128)(2,1)}) custom-call(bf16[32,40,512]{2,1,0:T(8,128)(2,1)} %bitcast.7, bf16[32,8,640]{2,1,0:T(8,128)(2,1)} %get-tuple-element.16.g_ref), custom_call_target="tpu_custom_call" | custom-call | tf_op jit(solution)/shard_map/give_back/pallas_call | solution.py:414
  99.4 6.6 %mix.1 = bf16[2,4,24,640]{3,2,1,0:T(8,128)(2,1)} custom-call(bf16[16,2,40,512]{3,2,1,0:T(8,128)(2,1)} %bitcast.8, bf16[16,16,2,8,640]{4,3,2,1,0:T(8,128)(2,1)} %bitcast.6), custom_call_target="tpu_custom_call" | custom-call | tf_op jit(solution)/shard_map/mix/pallas_call | solution.py:425

commit v2 on v0

v2 whole, which is shorter than its diff:
```python
import jax
import jax.numpy as jnp
from jax import lax
from jax.experimental import pallas as pl
from jax.experimental.pallas import tpu as pltpu
from jax.sharding import PartitionSpec as P

MESH = pl.DeviceIdType.MESH
F32 = jnp.float32
BF16 = jnp.bfloat16
NLAT, NLON = 16, 32


def remote(src, dst, send, recv, where):
    return pltpu.make_async_remote_copy(
        src_ref=src,
        dst_ref=dst,
        send_sem=send,
        recv_sem=recv,
        device_id=where,
        device_id_type=MESH,
    )


def layer_kernel(
    low_ref, shift_ref, f_ref, w_ref, k_hbm, ra_ref, ga_ref,
    k_ref, m_ref, wp_ref, r_ref, rh_ref, g_ref, ku_ref, kh_ref,
    x_ref, lhs_ref, rhs_ref, acc_ref, a_ref, sp_ref, sq_ref,
    m_send, m_recv, w_send, w_recv, a_send, a_recv,
    h_send, h_recv, k_send, k_recv, c_send, c_recv, s_send, s_recv, own_sem,
):
    lat = lax.axis_index("lat")
    lon = lax.axis_index("lon")
    up, down = lax.rem(lat + 1, NLAT), lax.rem(lat + NLAT - 1, NLAT)
    up2, down2 = lax.rem(lat + 2, NLAT), lax.rem(lat + NLAT - 2, NLAT)
    twin = lat + 1 - 2 * lax.rem(lat, 2)
    first = 4 * lat
    barrier = pltpu.get_barrier_semaphore()

    def peer(j):
        return lax.rem(lon + j, NLON)

    def greet(j, c):
        pl.semaphore_signal(barrier, inc=1, device_id={"lon": peer(j)}, device_id_type=MESH)
        return c

    lax.fori_loop(1, NLON, greet, 0)
    for other in (up, down, up2, down2):
        pl.semaphore_signal(barrier, inc=1, device_id={"lat": other}, device_id_type=MESH)
    k_copy = pltpu.make_async_copy(k_hbm, k_ref, own_sem.at[0])
    k_copy.start()

    rows = [f_ref[:, r].astype(F32).reshape(48, 640) for r in range(4)]
    gap = jnp.zeros((48, 48), F32)
    for g in range(16):
        cut = [row[:, 40 * g : 40 * g + 40] for row in rows]
        packed = jnp.concatenate([cut[0], cut[1], gap, cut[2], cut[3], gap], axis=1)
        m_ref[2 * g] = packed[0:24].astype(BF16)
        m_ref[2 * g + 1] = packed[24:48].astype(BF16)
    odd = lax.rem(lon, 2) == 1
    four = jnp.zeros((4, 640), F32)
    for k in range(5):
        w = w_ref[k].astype(F32)
        padded = jnp.where(
            odd,
            jnp.concatenate([four, w], axis=0),
            jnp.concatenate([w, four], axis=0),
        )
        for n in range(3):
            wp_ref[3 * k + n] = padded[8 * n : 8 * n + 8].astype(BF16)
    wp_ref[15] = jnp.zeros((8, 640), BF16)

    q = lax.broadcasted_iota(jnp.int32, (64, 256), 0)
    lane = lax.broadcasted_iota(jnp.int32, (64, 256), 1)
    base = 32 * (q >> 3) + (q & 7)
    for o in range(4):
        spread = jnp.where(lane == base + 8 * o, 1.0, 0.0).astype(BF16)
        sp_ref[o] = spread
        sq_ref[o // 2, 64 * (o % 2) : 64 * (o % 2) + 64] = spread
    sp_ref[4] = jnp.zeros((64, 256), BF16)

    k_copy.wait()

    def pack_halo(k, c):
        for side in range(2):
            for n in range(2):
                r = 2 * (1 - side) + n
                low = low_ref[k, first + r]
                inside = (lat < NLAT - 1) if side == 0 else (lat > 0)
                halves = []
                for o in range(2):
                    t = o + 2 - n - low if side == 0 else o - 2 - n - low
                    good = (t >= 0) & (t < 3) & inside
                    block = k_ref[k, r, jnp.clip(t, 0, 2)].reshape(192, 64).astype(F32)
                    halves.append(jnp.where(good, block, 0.0))
                ku_ref[side, k, n] = jnp.concatenate(halves, axis=1).astype(BF16)
        return c

    lax.fori_loop(0, 5, pack_halo, 0)

    pl.semaphore_wait(barrier, NLON + 3)

    def send_m(j):
        to = peer(j)
        return remote(m_ref.at[to], r_ref.at[lon], m_send.at[to], m_recv.at[lon], {"lon": to})

    def send_w(j):
        to = peer(j)
        return remote(wp_ref.at[lat], g_ref.at[lon], w_send.at[to], w_recv.at[lon], {"lon": to})

    def send_a(to):
        return remote(a_ref.at[to], ra_ref.at[lon], a_send.at[to], a_recv.at[lon], {"lon": to})

    def start_m(j, c):
        send_m(j).start()
        return c

    def start_w(j, c):
        send_w(j).start()
        return c

    lax.fori_loop(1, NLON, start_m, 0)
    own_m = pltpu.make_async_copy(m_ref.at[lon], r_ref.at[lon], own_sem.at[1])
    own_w = pltpu.make_async_copy(wp_ref.at[lat], g_ref.at[lon], own_sem.at[2])
    own_m.start()
    own_w.start()
    k_up = remote(ku_ref.at[0], kh_ref.at[0], k_send.at[0], k_recv.at[0], {"lat": up})
    k_down = remote(ku_ref.at[1], kh_ref.at[1], k_send.at[1], k_recv.at[1], {"lat": down})
    k_up.start()
    k_down.start()
    lax.fori_loop(1, NLON, start_w, 0)

    def own_rows(k, c):
        for r in range(4):
            low = low_ref[k, first + r]
            total = jnp.zeros((192, 256), F32)
            for t in range(3):
                o = r + low + t
                slot = jnp.where((o >= 0) & (o < 4), o, 4)
                total = total + jnp.dot(
                    k_ref[k, r, t].reshape(192, 64), sp_ref[slot], preferred_element_type=F32
                )
            at = 256 * (r + 2)
            rhs_ref[k, at : at + 192] = total.astype(BF16)
        for i in range(8):
            rhs_ref[k, 256 * i + 192 : 256 * i + 256] = jnp.zeros((64, 256), BF16)
        return c

    lax.fori_loop(0, 5, own_rows, 0)

    def take_m(j, c):
        src = lax.rem(lon + NLON - j, NLON)
        remote(
            m_ref.at[lon], r_ref.at[src], m_send.at[src], m_recv.at[src], {"lon": src}
        ).wait_recv()
        return c

    own_m.wait()
    lax.fori_loop(1, NLON, take_m, 0)
    h_up = remote(
        r_ref.at[:, :, pl.ds(128, 128)], rh_ref.at[0], h_send.at[0], h_recv.at[0], {"lat": up}
    )
    h_down = remote(
        r_ref.at[:, :, pl.ds(0, 128)], rh_ref.at[1], h_send.at[1], h_recv.at[1], {"lat": down}
    )
    h_up.start()
    h_down.start()

    left80 = lax.broadcasted_iota(jnp.int32, (80, 128), 1) < 64
    left40 = lax.broadcasted_iota(jnp.int32, (40, 128), 1) < 64

    def turn(slot, load):
        for u in range(2):
            cells = load(16 * u).astype(F32).reshape(384, 128)
            for p in range(3):
                t = cells[128 * p : 128 * p + 128].T[0:80]
                s = pltpu.roll(t, 64, 1)
                x_ref[slot, 6 * u + 2 * p] = jnp.where(left80, t, s)
                x_ref[slot, 6 * u + 2 * p + 1] = jnp.where(left80, s, t)

    def gather(rows):
        for i in rows:
            row = jnp.clip(first - 2 + i, 0, 63)
            shifts = [shift_ref[j, row] + 12 for j in range(3)]
            part = slice(40 * (i % 2), 40 * (i % 2) + 40)

            def group(x, c, i=i, shifts=shifts, part=part):
                out = []
                for b in range(3):
                    x0, x1, x2 = [
                        x_ref[i // 2, lax.rem(3 * x + b + s, 12), part] for s in shifts
                    ]
                    out.append(jnp.concatenate([jnp.where(left40, x0, x1), x2], axis=1))
                lhs_ref[x, :, 256 * i : 256 * i + 256] = jnp.concatenate(out, axis=0).astype(BF16)
                return c

            lax.fori_loop(0, 4, group, 0)

    turn(1, lambda u: r_ref[u : u + 16, :, 0:128])
    turn(2, lambda u: r_ref[u : u + 16, :, 128:256])
    gather((2, 3, 4, 5))

    k_up.wait_recv()
    k_down.wait_recv()

    def halo_rows(k, c):
        for side in range(2):
            for n in range(2):
                at = 256 * (6 * side + n)
                rhs_ref[k, at : at + 192] = jnp.dot(
                    kh_ref[side, k, n], sq_ref[side], preferred_element_type=F32
                ).astype(BF16)
        return c

    lax.fori_loop(0, 5, halo_rows, 0)

    h_up.wait_recv()
    h_down.wait_recv()
    turn(0, lambda u: rh_ref[0, u : u + 16])
    turn(3, lambda u: rh_ref[1, u : u + 16])
    gather((0, 1, 6, 7))

    def above(n, start):
        return lax.rem(start + 2 * n, NLAT)

    def below(n, start):
        return lax.rem(start + 2 * NLAT - 2 * n, NLAT)

    started = []

    def go(copy):
        copy.start()
        started.append(copy)

    def ring_up(n):
        src = g_ref if n == 0 else ga_ref.at[below(n, lat)]
        return remote(
            src, ga_ref.at[below(n, lat)], c_send.at[n], c_recv.at[n], {"lat": up2}
        )

    def ring_down(n):
        src = g_ref if n == 0 else ga_ref.at[above(n, lat)]
        return remote(
            src, ga_ref.at[above(n, lat)], c_send.at[4 + n], c_recv.at[4 + n], {"lat": down2}
        )

    def to_twin(slot, piece, src):
        return remote(src, ga_ref.at[piece], s_send.at[slot], s_recv.at[slot], {"lat": twin})

    def ring_step(n):
        piece = below(n, lat)
        remote(
            g_ref, ga_ref.at[piece], c_send.at[n - 1], c_recv.at[n - 1], {"lat": up2}
        ).wait_recv()
        if n < 4:
            go(ring_up(n))
        go(to_twin(n, piece, ga_ref.at[piece]))
        if n < 4:
            piece = above(n, lat)
            remote(
                g_ref, ga_ref.at[piece], c_send.at[3 + n], c_recv.at[3 + n], {"lat": down2}
            ).wait_recv()
            if n < 3:
                go(ring_down(n))
            go(to_twin(4 + n, piece, ga_ref.at[piece]))

    def take_w(j, c):
        src = lax.rem(lon + NLON - j, NLON)
        remote(
            wp_ref.at[lat], g_ref.at[src], w_send.at[src], w_recv.at[src], {"lon": src}
        ).wait_recv()
        return c

    tail = jnp.zeros((40, 32), F32)
    own_x, own_y = lon // 8, lax.rem(lon, 8)
    own_a = pltpu.make_async_copy(a_ref.at[lon], ra_ref.at[lon], own_sem.at[3])
    own_g = pltpu.make_async_copy(g_ref, ga_ref.at[lat], own_sem.at[4])
    for step in range(4):
        x = lax.rem(own_x + step, 4)

        def basis(k, c, x=x):
            acc_ref[k] = jnp.dot(lhs_ref[x], rhs_ref[k], preferred_element_type=F32)
            return c

        lax.fori_loop(0, 5, basis, 0)
        for y in range(8):
            groups = [divmod(3 * y + n, 8) for n in range(3)]
            parts = []
            for k in range(5):
                n = 0
                while n < 3:
                    beta, qg = groups[n]
                    m = n
                    while m < 3 and groups[m][0] == beta:
                        m += 1
                    parts.append(
                        acc_ref[k, 40 * beta : 40 * beta + 40, 32 * qg : 32 * (qg + m - n)]
                    )
                    n = m
            a_ref[8 * x + y] = jnp.concatenate(parts + [tail], axis=1).astype(BF16)

        def start_a(n, c, x=x):
            send_a(8 * x + lax.rem(own_y + n, 8)).start()
            return c

        lax.fori_loop(1 if step == 0 else 0, 8, start_a, 0)
        if step == 0:
            own_a.start()
            own_w.wait()
            lax.fori_loop(1, NLON, take_w, 0)
            go(ring_up(0))
            go(ring_down(0))
            own_g.start()
            go(to_twin(0, lat, g_ref))
        elif step > 1:
            ring_step(step - 1)
    ring_step(3)
    ring_step(4)

    def finish(j, c):
        src = lax.rem(lon + NLON - j, NLON)
        remote(
            a_ref.at[lon], ra_ref.at[src], a_send.at[src], a_recv.at[src], {"lon": src}
        ).wait_recv()
        send_a(peer(j)).wait_send()
        send_m(j).wait_send()
        send_w(j).wait_send()
        return c

    lax.fori_loop(1, NLON, finish, 0)
    for slot in range(8):
        piece = below(slot, twin) if slot < 5 else above(slot - 4, twin)
        remote(
            g_ref, ga_ref.at[piece], s_send.at[slot], s_recv.at[slot], {"lat": twin}
        ).wait_recv()
    for copy in started + [k_up, k_down, h_up, h_down]:
        copy.wait_send()
    own_a.wait()
    own_g.wait()


def mix_kernel(ra_ref, g_ref, o_ref, t_ref, acc_ref):
    k = pl.program_id(0)

    @pl.when(k == 0)
    def _():
        for e in range(2):
            a = ra_ref[:, e].astype(F32).reshape(640, 512)
            t_ref[e] = a.T.astype(BF16)
        acc_ref[...] = jnp.zeros_like(acc_ref)

    def part(r, h):
        return g_ref[r, :, h].astype(F32)

    w = jnp.stack(
        [part(0, 0), part(1, 0), part(2, 0) + part(0, 1), part(1, 1), part(2, 1)], axis=1
    )
    w = w.reshape(640, 640).astype(BF16)
    rows = pl.ds(pl.multiple_of(96 * k, 32), 96)
    for e in range(2):
        acc_ref[e] += jnp.dot(t_ref[e, rows], w, preferred_element_type=F32)

    @pl.when(k == 4)
    def _():
        for e in range(2):
            v = acc_ref[e].reshape(3, 4, 8, 640)
            v = v * (1.0 + lax.erf(v * 0.7071067811865476)) * 0.5
            for o in range(4):
                o_ref[e, o] = v[:, o].reshape(24, 640).astype(BF16)


def per_device(fields, kernel, band_low, block_shift, mix_weight):
    whole = pl.BlockSpec(memory_space=pltpu.VMEM)
    smem = pl.BlockSpec(memory_space=pltpu.SMEM)
    anywhere = pl.BlockSpec(memory_space=pl.ANY)
    shape = jax.ShapeDtypeStruct
    dma = pltpu.SemaphoreType.DMA
    vmem = pltpu.VMEM

    returned, weights = pl.pallas_call(
        layer_kernel,
        out_shape=(shape((32, 40, 512), BF16), shape((16, 32, 8, 640), BF16)),
        in_specs=[smem, smem, whole, whole, anywhere],
        out_specs=(anywhere,) * 2,
        scratch_shapes=[
            vmem((5, 4, 3, 3, 64, 64), BF16),
            vmem((32, 24, 256), BF16),
            vmem((16, 8, 640), BF16),
            vmem((32, 24, 256), BF16),
            vmem((2, 32, 24, 128), BF16),
            vmem((32, 8, 640), BF16),
            vmem((2, 5, 2, 192, 128), BF16),
            vmem((2, 5, 2, 192, 128), BF16),
            vmem((4, 12, 80, 128), F32),
            vmem((4, 120, 2048), BF16),
            vmem((5, 2048, 256), BF16),
            vmem((5, 120, 256), F32),
            vmem((32, 40, 512), BF16),
            vmem((5, 64, 256), BF16),
            vmem((2, 128, 256), BF16),
            dma((32,)), dma((32,)), dma((32,)), dma((32,)), dma((32,)), dma((32,)),
            dma((2,)), dma((2,)), dma((2,)), dma((2,)),
            dma((7,)), dma((7,)), dma((8,)), dma((8,)), dma((5,)),
        ],
        compiler_params=pltpu.CompilerParams(collective_id=0, has_side_effects=True),
        name="layer",
    )(
        band_low,
        block_shift.T,
        jnp.transpose(fields, (0, 1, 3, 2)),
        mix_weight,
        kernel,
    )
    return pl.pallas_call(
        mix_kernel,
        out_shape=shape((2, 4, 24, 640), BF16),
        grid=(5,),
        in_specs=[
            pl.BlockSpec((16, 2, 40, 512), lambda k: (0, 0, 0, 0)),
            pl.BlockSpec((3, 16, 2, 8, 640), lambda k: (k, 0, 0, 0, 0)),
        ],
        out_specs=pl.BlockSpec((2, 4, 24, 640), lambda k: (0, 0, 0, 0)),
        scratch_shapes=[pltpu.VMEM((2, 512, 640), BF16), pltpu.VMEM((2, 96, 640), F32)],
        name="mix",
    )(returned.reshape(16, 2, 40, 512), weights.reshape(16, 16, 2, 8, 640))


def solution(mesh):
    placed = (
        P(None, "lat", None, "lon"),
        P(None, "lat", None, None, None, None),
        P(),
        P(),
        P(None, "lon", None),
    )
    return jax.shard_map(
        per_device,
        mesh=mesh,
        in_specs=placed,
        out_specs=P(None, "lat", "lon", None),
        check_vma=False,
    )
```

time: 246 us -> 81.8 us (0.33)
  the two profiles are of different devices: /device:TPU:264 before, /device:TPU:1 now
where the time goes in v2:
time: 81.8 us; the launch traced here: 81.5 us
  Pallas kernels  81.5 us (100%)
    pallas_call x1, Pallas kernels, per_device(): pl.pallas_call(layer_kernel, out_shape=(shape((32, 40, 512), BF16), shape...  74.9 us
    pallas_call x1, Pallas kernels, per_device(): pl.pallas_call(mix_kernel, out_shape=shape((2, 4, 24, 640), BF16), grid=(...  6.63 us

profile of v2, /device:TPU:1, one launch (start us, length us, event | category | flops | bytes accessed | tf_op | source)
XLA Modules:
  0.0 81.5 jit_solution(12285988992719588528)
XLA Ops:
  0.0 74.9 %layer.1 = (bf16[32,40,512]{2,1,0:T(8,128)(2,1)}, bf16[16,32,8,640]{3,2,1,0:T(8,128)(2,1)}) custom-call(s32[5,64]{1,0:T(8,128)} %low_ref.1, s32[3,64]{1,0:T(4,128)} %bitcast.7, bf16[2,4,24,640]{3,2,1,0:T(8,128)(2,1)} %bitcast.6, bf16[5,20,640]{2,1,0:T(8,128)(2,1)} %w_ref.1, bf16[5,4,3,3,64,64]{5,4,3,2,1,0:T(8,128)(2,1)} %k_hbm.1), custom_call_target="tpu_custom_call" | custom-call | tf_op jit(solution)/shard_map/layer/pallas_call | solution.py:380
  74.9 6.6 %mix.1 = bf16[2,4,24,640]{3,2,1,0:T(8,128)(2,1)} custom-call(bf16[16,2,40,512]{3,2,1,0:T(8,128)(2,1)} %bitcast.5, bf16[16,16,2,8,640]{4,3,2,1,0:T(8,128)(2,1)} %bitcast.4), custom_call_target="tpu_custom_call" | custom-call | tf_op jit(solution)/shard_map/mix/pallas_call | solution.py:414

commit v3 on v2

v3 whole, which is shorter than its diff:
```python
import jax
import jax.numpy as jnp
from jax import lax
from jax.experimental import pallas as pl
from jax.experimental.pallas import tpu as pltpu
from jax.sharding import PartitionSpec as P

MESH = pl.DeviceIdType.MESH
F32 = jnp.float32
BF16 = jnp.bfloat16
NLAT, NLON = 16, 32


def remote(src, dst, send, recv, where):
    return pltpu.make_async_remote_copy(
        src_ref=src,
        dst_ref=dst,
        send_sem=send,
        recv_sem=recv,
        device_id=where,
        device_id_type=MESH,
    )


def layer_kernel(
    low_ref, shift_ref, f_hbm, w_hbm, k_hbm, o_ref,
    f_ref, w_ref, k_ref, m_ref, wp_ref, r_ref, rh_ref, g_ref, ku_ref, kh_ref,
    x_ref, lhs_ref, rhs_ref, acc_ref, a_ref, sp_ref, sq_ref,
    ra_ref, ga_ref, wv_ref, t_ref, sum_ref,
    m_send, m_recv, y_send, y_recv, b_send, b_recv, a_send, a_recv,
    h_send, h_recv, k_send, k_recv, c_send, c_recv, s_send, s_recv, own_sem,
):
    lat = lax.axis_index("lat")
    lon = lax.axis_index("lon")
    up, down = lax.rem(lat + 1, NLAT), lax.rem(lat + NLAT - 1, NLAT)
    up2, down2 = lax.rem(lat + 2, NLAT), lax.rem(lat + NLAT - 2, NLAT)
    twin = lat + 1 - 2 * lax.rem(lat, 2)
    first = 4 * lat
    barrier = pltpu.get_barrier_semaphore()

    def peer(j):
        return lax.rem(lon + j, NLON)

    def greet(j, c):
        pl.semaphore_signal(barrier, inc=1, device_id={"lon": peer(j)}, device_id_type=MESH)
        return c

    lax.fori_loop(1, NLON, greet, 0)
    for other in (up, down, up2, down2):
        pl.semaphore_signal(barrier, inc=1, device_id={"lat": other}, device_id_type=MESH)
    f_copy = pltpu.make_async_copy(f_hbm, f_ref, own_sem.at[5])
    w_copy = pltpu.make_async_copy(w_hbm, w_ref, own_sem.at[6])
    k_copy = pltpu.make_async_copy(k_hbm, k_ref, own_sem.at[0])
    f_copy.start()
    w_copy.start()
    k_copy.start()
    f_copy.wait()

    rows = [f_ref[:, r].astype(F32).reshape(48, 640) for r in range(4)]
    gap48 = jnp.zeros((48, 8), F32)
    gap8 = jnp.zeros((8, 8), F32)
    for g in range(16):
        cut = [row[:, 40 * g : 40 * g + 40] for row in rows]
        packed = jnp.concatenate([cut[0], cut[1], cut[2], gap48], axis=1)
        for e in range(2):
            last = [cut[3][24 * e + 8 * n : 24 * e + 8 * n + 8] for n in range(3)]
            both = [packed[24 * e : 24 * e + 24], jnp.concatenate(last + [gap8], axis=1)]
            m_ref[2 * g + e] = jnp.concatenate(both, axis=0).astype(BF16)
    w_copy.wait()
    odd = lax.rem(lon, 2) == 1
    four = jnp.zeros((4, 640), F32)
    for k in range(5):
        w = w_ref[k].astype(F32)
        padded = jnp.where(
            odd,
            jnp.concatenate([four, w], axis=0),
            jnp.concatenate([w, four], axis=0),
        )
        for n in range(3):
            wp_ref[3 * k + n] = padded[8 * n : 8 * n + 8].astype(BF16)
    wp_ref[15] = jnp.zeros((8, 640), BF16)

    pl.semaphore_wait(barrier, NLON + 3)

    def send_m(j):
        to = peer(j)
        return remote(m_ref.at[to], r_ref.at[lon], m_send.at[to], m_recv.at[lon], {"lon": to})

    def send_a(to):
        return remote(a_ref.at[to], ra_ref.at[lon], a_send.at[to], a_recv.at[lon], {"lon": to})

    def start_m(j, c):
        send_m(j).start()
        return c

    own_x, own_y = lon // 8, lax.rem(lon, 8)
    w_started = []

    def w_go(copy):
        copy.start()
        w_started.append(copy)

    def y_copy(d, at):
        to = 8 * own_x + lax.rem(own_y + d, 8)
        return remote(wp_ref.at[lat], g_ref.at[at], y_send.at[d], y_recv.at[d], {"lon": to})

    def x_block(d, x):
        block = g_ref.at[pl.ds(pl.multiple_of(8 * x, 8), 8)]
        to = 8 * lax.rem(own_x + d, 4) + own_y
        return remote(block, block, b_send.at[d], b_recv.at[d], {"lon": to})

    for d in range(1, 8):
        w_go(y_copy(d, lon))
    lax.fori_loop(1, NLON, start_m, 0)
    own_m = pltpu.make_async_copy(m_ref.at[lon], r_ref.at[lon], own_sem.at[1])
    own_w = pltpu.make_async_copy(wp_ref.at[lat], g_ref.at[lon], own_sem.at[2])
    own_m.start()
    own_w.start()
    q = lax.broadcasted_iota(jnp.int32, (64, 256), 0)
    lane = lax.broadcasted_iota(jnp.int32, (64, 256), 1)
    base = 32 * (q >> 3) + (q & 7)
    for o in range(4):
        spread = jnp.where(lane == base + 8 * o, 1.0, 0.0).astype(BF16)
        sp_ref[o] = spread
        sq_ref[o // 2, 64 * (o % 2) : 64 * (o % 2) + 64] = spread
    sp_ref[4] = jnp.zeros((64, 256), BF16)

    k_copy.wait()

    def pack_halo(k, c):
        for side in range(2):
            for n in range(2):
                r = 2 * (1 - side) + n
                low = low_ref[k, first + r]
                inside = (lat < NLAT - 1) if side == 0 else (lat > 0)
                halves = []
                for o in range(2):
                    t = o + 2 - n - low if side == 0 else o - 2 - n - low
                    good = (t >= 0) & (t < 3) & inside
                    block = k_ref[k, r, jnp.clip(t, 0, 2)].reshape(192, 64).astype(F32)
                    halves.append(jnp.where(good, block, 0.0))
                ku_ref[side, k, n] = jnp.concatenate(halves, axis=1).astype(BF16)
        return c

    lax.fori_loop(0, 5, pack_halo, 0)
    k_up = remote(ku_ref.at[0], kh_ref.at[0], k_send.at[0], k_recv.at[0], {"lat": up})
    k_down = remote(ku_ref.at[1], kh_ref.at[1], k_send.at[1], k_recv.at[1], {"lat": down})
    k_up.start()
    k_down.start()

    def own_rows(k, c):
        for r in range(4):
            low = low_ref[k, first + r]
            total = jnp.zeros((192, 256), F32)
            for t in range(3):
                o = r + low + t
                slot = jnp.where((o >= 0) & (o < 4), o, 4)
                total = total + jnp.dot(
                    k_ref[k, r, t].reshape(192, 64), sp_ref[slot], preferred_element_type=F32
                )
            at = 256 * (r + 2)
            rhs_ref[k, at : at + 192] = total.astype(BF16)
        for i in range(8):
            rhs_ref[k, 256 * i + 192 : 256 * i + 256] = jnp.zeros((64, 256), BF16)
        return c

    lax.fori_loop(0, 5, own_rows, 0)

    own_w.wait()
    for d in range(1, 8):
        y_copy(d, 8 * own_x + lax.rem(own_y + 8 - d, 8)).wait_recv()
    for d in range(1, 4):
        w_go(x_block(d, own_x))

    def hand_on(src):
        remote(
            r_ref.at[src], rh_ref.at[0, src], h_send.at[0], h_recv.at[0], {"lat": up}
        ).start()
        remote(
            r_ref.at[src], rh_ref.at[1, src], h_send.at[1], h_recv.at[1], {"lat": down}
        ).start()

    def take_m(j, c):
        src = lax.rem(lon + NLON - j, NLON)
        remote(
            m_ref.at[lon], r_ref.at[src], m_send.at[src], m_recv.at[src], {"lon": src}
        ).wait_recv()
        hand_on(src)
        return c

    own_m.wait()
    hand_on(lon)
    lax.fori_loop(1, NLON, take_m, 0)
    h_up = remote(r_ref, rh_ref.at[0], h_send.at[0], h_recv.at[0], {"lat": up})
    h_down = remote(r_ref, rh_ref.at[1], h_send.at[1], h_recv.at[1], {"lat": down})

    left40 = lax.broadcasted_iota(jnp.int32, (40, 128), 1) < 64

    def turn(load, first_row, wanted):
        def put(cells, u, picks):
            for p in range(3):
                t = cells[128 * p : 128 * p + 128].T
                for r, at in picks:
                    v = t[at : at + 40]
                    w = pltpu.roll(v, 64, 1)
                    x_ref[first_row + r, 6 * u + 2 * p] = jnp.where(left40, v, w)
                    x_ref[first_row + r, 6 * u + 2 * p + 1] = jnp.where(left40, w, v)

        for u in range(2):
            both = load(16 * u).astype(F32)
            picks = [(r, 40 * r) for r in wanted if r < 3]
            put(both[:, 0:24].reshape(384, 128), u, picks)
            if 3 in wanted:
                last = both[:, 24:32].reshape(128, 128)
                turned = [last, pltpu.roll(last, 88, 1), pltpu.roll(last, 48, 1)]
                cells = jnp.stack([v.reshape(16, 8, 128) for v in turned], axis=1)
                put(cells.reshape(384, 128), u, [(3, 0)])

    def gather(rows):
        for i in rows:
            row = jnp.clip(first - 2 + i, 0, 63)
            shifts = [shift_ref[j, row] + 12 for j in range(3)]

            def group(x, c, i=i, shifts=shifts):
                out = []
                for b in range(3):
                    x0, x1, x2 = [x_ref[i, lax.rem(3 * x + b + s, 12)] for s in shifts]
                    out.append(jnp.concatenate([jnp.where(left40, x0, x1), x2], axis=1))
                lhs_ref[x, :, 256 * i : 256 * i + 256] = jnp.concatenate(out, axis=0).astype(BF16)
                return c

            lax.fori_loop(0, 4, group, 0)

    turn(lambda u: r_ref[u : u + 16], 2, (0, 1, 2, 3))
    gather((2, 3, 4, 5))

    def above(n, start):
        return lax.rem(start + 2 * n, NLAT)

    def below(n, start):
        return lax.rem(start + 2 * NLAT - 2 * n, NLAT)

    started = []

    def go(copy):
        copy.start()
        started.append(copy)

    def part(n, at, half):
        return ga_ref.at[at] if n < 3 else ga_ref.at[at, pl.ds(16 * half, 16)]

    def ring_up(n):
        dst = part(n, below(n, lat), 0)
        return remote(g_ref if n == 0 else dst, dst, c_send.at[n], c_recv.at[n], {"lat": up2})

    def ring_down(n):
        dst = part(n, above(n, lat), 1)
        return remote(
            g_ref if n == 0 else dst, dst, c_send.at[4 + n], c_recv.at[4 + n], {"lat": down2}
        )

    def to_twin(slot, piece, src):
        return remote(src, ga_ref.at[piece], s_send.at[slot], s_recv.at[slot], {"lat": twin})

    def ring_step(n):
        piece = below(n, lat)
        came = part(n - 1, piece, 0)
        remote(came, came, c_send.at[n - 1], c_recv.at[n - 1], {"lat": up2}).wait_recv()
        if n < 4:
            go(ring_up(n))
            go(to_twin(n, piece, ga_ref.at[piece]))
        other = above(n, lat)
        came = part(n - 1, other, 1)
        remote(came, came, c_send.at[3 + n], c_recv.at[3 + n], {"lat": down2}).wait_recv()
        if n < 4:
            go(ring_down(n))
            go(to_twin(4 + n, other, ga_ref.at[other]))
        else:
            go(to_twin(n, piece, ga_ref.at[piece]))

    for d in range(1, 4):
        x_block(d, lax.rem(own_x + 4 - d, 4)).wait_recv()
    own_g = pltpu.make_async_copy(g_ref, ga_ref.at[lat], own_sem.at[4])
    go(ring_up(0))
    go(ring_down(0))
    own_g.start()
    go(to_twin(0, lat, g_ref))

    k_up.wait_recv()
    k_down.wait_recv()

    def halo_rows(k, c):
        for side in range(2):
            for n in range(2):
                at = 256 * (6 * side + n)
                rhs_ref[k, at : at + 192] = jnp.dot(
                    kh_ref[side, k, n], sq_ref[side], preferred_element_type=F32
                ).astype(BF16)
        return c

    lax.fori_loop(0, 5, halo_rows, 0)

    h_up.wait_recv()
    h_down.wait_recv()
    turn(lambda u: rh_ref[0, u : u + 16], -2, (2, 3))
    turn(lambda u: rh_ref[1, u : u + 16], 6, (0, 1))
    gather((0, 1, 6, 7))
    tail = jnp.zeros((40, 32), F32)
    own_a = pltpu.make_async_copy(a_ref.at[lon], ra_ref.at[lon], own_sem.at[3])
    for step in range(4):
        x = lax.rem(own_x + step, 4)

        def basis(k, c, x=x):
            acc_ref[k] = jnp.dot(lhs_ref[x], rhs_ref[k], preferred_element_type=F32)
            return c

        lax.fori_loop(0, 5, basis, 0)
        for y in range(8):
            groups = [divmod(3 * y + n, 8) for n in range(3)]
            parts = []
            for k in range(5):
                n = 0
                while n < 3:
                    beta, qg = groups[n]
                    m = n
                    while m < 3 and groups[m][0] == beta:
                        m += 1
                    parts.append(
                        acc_ref[k, 40 * beta : 40 * beta + 40, 32 * qg : 32 * (qg + m - n)]
                    )
                    n = m
            a_ref[8 * x + y] = jnp.concatenate(parts + [tail], axis=1).astype(BF16)

        def start_a(n, c, x=x):
            send_a(8 * x + lax.rem(own_y + n, 8)).start()
            return c

        lax.fori_loop(1 if step == 0 else 0, 8, start_a, 0)
        if step == 0:
            own_a.start()
        elif step == 1:
            ring_step(1)
    for n in range(2, 5):
        ring_step(n)

    for slot in range(8):
        piece = below(slot, twin) if slot < 5 else above(slot - 4, twin)
        remote(
            g_ref, ga_ref.at[piece], s_send.at[slot], s_recv.at[slot], {"lat": twin}
        ).wait_recv()
    own_g.wait()

    def order(n, c):
        k, x = n // 4, lax.rem(n, 4)
        piece = [
            ga_ref[3 * k + r, pl.ds(pl.multiple_of(8 * x, 8), 8)].astype(F32).reshape(4, 2, 8, 640)
            for r in range(3)
        ]
        even = [v[:, 0] for v in piece]
        odds = [v[:, 1] for v in piece]
        w = jnp.stack([even[0], even[1], even[2] + odds[0], odds[1], odds[2]], axis=1)
        w = jnp.concatenate([w.reshape(160, 640), jnp.zeros((96, 640), F32)], axis=0)
        wv_ref[x, pl.ds(pl.multiple_of(256 * k, 256), 256)] = w.astype(BF16)
        return c

    lax.fori_loop(0, 20, order, 0)

    for step in range(4):
        x = lax.rem(own_x + 4 - step, 4)

        def take_a(n, c, x=x):
            src = 8 * x + lax.rem(own_y + n, 8)
            remote(
                a_ref.at[lon], ra_ref.at[src], a_send.at[src], a_recv.at[src], {"lon": src}
            ).wait_recv()
            return c

        lax.fori_loop(1 if step == 0 else 0, 8, take_a, 0)
        if step == 0:
            own_a.wait()
        for e in range(2):
            parts = [ra_ref[8 * x + 2 * g + e].astype(F32) for g in range(4)]
            turned = jnp.concatenate(parts + [jnp.zeros((96, 512), F32)], axis=0).T.astype(BF16)
            for k in range(5):
                t_ref[96 * e : 96 * e + 96, 256 * k : 256 * k + 256] = turned[
                    96 * k : 96 * k + 96
                ]
        now = jnp.dot(t_ref[...], wv_ref[x], preferred_element_type=F32)
        if step == 0:
            sum_ref[...] = now
        elif step < 3:
            sum_ref[...] += now
        else:
            v = sum_ref[...] + now
            v = (v * (1.0 + lax.erf(v * 0.7071067811865476)) * 0.5).reshape(2, 3, 4, 8, 640)
            for e in range(2):
                for o in range(4):
                    o_ref[e, o] = v[e, :, o].reshape(24, 640).astype(BF16)

    def finish(j, c):
        send_a(peer(j)).wait_send()
        send_m(j).wait_send()
        return c

    lax.fori_loop(1, NLON, finish, 0)
    for copy in started + w_started + [k_up, k_down, h_up, h_down]:
        copy.wait_send()


def per_device(fields, kernel, band_low, block_shift, mix_weight):
    whole = pl.BlockSpec(memory_space=pltpu.VMEM)
    smem = pl.BlockSpec(memory_space=pltpu.SMEM)
    anywhere = pl.BlockSpec(memory_space=pl.ANY)
    shape = jax.ShapeDtypeStruct
    dma = pltpu.SemaphoreType.DMA
    vmem = pltpu.VMEM

    return pl.pallas_call(
        layer_kernel,
        out_shape=shape((2, 4, 24, 640), BF16),
        in_specs=[smem, smem, anywhere, anywhere, anywhere],
        out_specs=whole,
        scratch_shapes=[
            vmem((2, 4, 24, 640), BF16),
            vmem((5, 20, 640), BF16),
            vmem((5, 4, 3, 3, 64, 64), BF16),
            vmem((32, 32, 128), BF16),
            vmem((16, 8, 640), BF16),
            vmem((32, 32, 128), BF16),
            vmem((2, 32, 32, 128), BF16),
            vmem((32, 8, 640), BF16),
            vmem((2, 5, 2, 192, 128), BF16),
            vmem((2, 5, 2, 192, 128), BF16),
            vmem((8, 12, 40, 128), F32),
            vmem((4, 120, 2048), BF16),
            vmem((5, 2048, 256), BF16),
            vmem((5, 120, 256), F32),
            vmem((32, 40, 512), BF16),
            vmem((5, 64, 256), BF16),
            vmem((2, 128, 256), BF16),
            vmem((32, 40, 512), BF16),
            vmem((16, 32, 8, 640), BF16),
            vmem((4, 1280, 640), BF16),
            vmem((192, 1280), BF16),
            vmem((192, 640), F32),
            dma((32,)), dma((32,)), dma((8,)), dma((8,)), dma((4,)), dma((4,)),
            dma((32,)), dma((32,)), dma((2,)), dma((2,)), dma((2,)), dma((2,)),
            dma((8,)), dma((8,)), dma((8,)), dma((8,)), dma((7,)),
        ],
        compiler_params=pltpu.CompilerParams(collective_id=0, has_side_effects=True),
        name="layer",
    )(
        band_low,
        block_shift.T,
        jnp.transpose(fields, (0, 1, 3, 2)),
        mix_weight,
        kernel,
    )

def solution(mesh):
    placed = (
        P(None, "lat", None, "lon"),
        P(None, "lat", None, None, None, None),
        P(),
        P(),
        P(None, "lon", None),
    )
    return jax.shard_map(
        per_device,
        mesh=mesh,
        in_specs=placed,
        out_specs=P(None, "lat", "lon", None),
        check_vma=False,
    )
```

time: 81.8 us -> 69 us (0.84)
  Pallas kernels: 81.5 us -> 67.1 us
  local copies, waits for them, and re-layouts: 0 us -> 1.66 us
    pallas_call x2 -> x1, Pallas kernels: 81.5 us -> 67.1 us  [per_device(): pl.pallas_call(layer_kernel, out_shape=shape((2, 4, 24, 640), BF16), in_s...]
    unnamed x0 -> x1, local copies, waits for them, and re-layouts: none -> 1.66 us
where the time goes in v3:
time: 69 us; the launch traced here: 68.8 us
  Pallas kernels  67.1 us (97%)
  local copies, waits for them, and re-layouts  1.66 us (2%)
    pallas_call x1, Pallas kernels, per_device(): pl.pallas_call(layer_kernel, out_shape=shape((2, 4, 24, 640), BF16), in_s...  67.1 us
    unnamed x1, local copies, waits for them, and re-layouts  1.66 us

profile of v3, /device:TPU:1, one launch (start us, length us, event | category | flops | bytes accessed | tf_op | source)
XLA Modules:
  0.0 68.8 jit_solution(12870250889730021995)
XLA Ops:
  0.0 67.1 %layer.1 = bf16[2,4,24,640]{3,2,1,0:T(8,128)(2,1)} custom-call(s32[5,64]{1,0:T(8,128)} %low_ref.1, s32[3,64]{1,0:T(4,128)} %bitcast.3, bf16[2,4,24,640]{3,2,1,0:T(8,128)(2,1)} %bitcast.2, bf16[5,20,640]{2,1,0:T(8,128)(2,1)} %w_hbm.1, bf16[5,4,3,3,64,64]{5,4,3,2,1,0:T(8,128)(2,1)} %k_hbm.1), custom_call_target="tpu_custom_call" | custom-call | tf_op jit(solution)/shard_map/layer/pallas_call | solution.py:418
  67.1 1.7 %copy.7 = bf16[2,4,24,640]{3,2,1,0:T(8,128)(2,1)} copy(bf16[2,4,24,640]{3,2,1,0:T(8,128)(2,1)} %layer.1) | data formatting | bytes 491520

commit v4 on v3

--- a/solution.py
+++ b/solution.py
@@ -1,3 +1,5 @@
+import functools
+
 import jax
 import jax.numpy as jnp
 from jax import lax
@@ -9,6 +11,7 @@
 F32 = jnp.float32
 BF16 = jnp.bfloat16
 NLAT, NLON = 16, 32
+FULL = (0, 2, 4, 6, 8, 10, 11, 12, 13, 14)
 
 
 def remote(src, dst, send, recv, where):
@@ -38,22 +41,23 @@
     first = 4 * lat
     barrier = pltpu.get_barrier_semaphore()
 
-    def peer(j):
-        return lax.rem(lon + j, NLON)
-
-    def greet(j, c):
-        pl.semaphore_signal(barrier, inc=1, device_id={"lon": peer(j)}, device_id_type=MESH)
-        return c
-
-    lax.fori_loop(1, NLON, greet, 0)
-    for other in (up, down, up2, down2):
-        pl.semaphore_signal(barrier, inc=1, device_id={"lat": other}, device_id_type=MESH)
     f_copy = pltpu.make_async_copy(f_hbm, f_ref, own_sem.at[5])
     w_copy = pltpu.make_async_copy(w_hbm, w_ref, own_sem.at[6])
     k_copy = pltpu.make_async_copy(k_hbm, k_ref, own_sem.at[0])
     f_copy.start()
     w_copy.start()
     k_copy.start()
+
+    def peer(j):
+        return lax.rem(lon + j, NLON)
+
+    def greet(j, c):
+        pl.semaphore_signal(barrier, inc=1, device_id={"lon": peer(j)}, device_id_type=MESH)
+        return c
+
+    lax.fori_loop(1, NLON, greet, 0)
+    for other in (up, down, up2, down2):
+        pl.semaphore_signal(barrier, inc=1, device_id={"lat": other}, device_id_type=MESH)
     f_copy.wait()
 
     rows = [f_ref[:, r].astype(F32).reshape(48, 640) for r in range(4)]
@@ -76,18 +80,20 @@
             jnp.concatenate([four, w], axis=0),
             jnp.concatenate([w, four], axis=0),
         )
-        for n in range(3):
-            wp_ref[3 * k + n] = padded[8 * n : 8 * n + 8].astype(BF16)
+        groups = [padded[8 * n : 8 * n + 8] for n in range(3)]
+        wp_ref[FULL[2 * k]] = jnp.where(odd, groups[1], groups[0]).astype(BF16)
+        wp_ref[FULL[2 * k + 1]] = jnp.where(odd, groups[2], groups[1]).astype(BF16)
+        wp_ref[2 * k + 1] = jnp.where(odd, groups[0], groups[2]).astype(BF16)
     wp_ref[15] = jnp.zeros((8, 640), BF16)
 
     pl.semaphore_wait(barrier, NLON + 3)
 
     def send_m(j):
         to = peer(j)
-        return remote(m_ref.at[to], r_ref.at[lon], m_send.at[to], m_recv.at[lon], {"lon": to})
-
-    def send_a(to):
-        return remote(a_ref.at[to], ra_ref.at[lon], a_send.at[to], a_recv.at[lon], {"lon": to})
+        return remote(m_ref.at[to], r_ref.at[lon], m_send.at[0], m_recv.at[lon], {"lon": to})
+
+    def send_a(to, step):
+        return remote(a_ref.at[to], ra_ref.at[lon], a_send.at[0], a_recv.at[step], {"lon": to})
 
     def start_m(j, c):
         send_m(j).start()
@@ -102,10 +108,11 @@
 
     def y_copy(d, at):
         to = 8 * own_x + lax.rem(own_y + d, 8)
-        return remote(wp_ref.at[lat], g_ref.at[at], y_send.at[d], y_recv.at[d], {"lon": to})
+        slot = g_ref.at[lax.rem(at, 2), at // 2]
+        return remote(wp_ref.at[lat], slot, y_send.at[d], y_recv.at[d], {"lon": to})
 
     def x_block(d, x):
-        block = g_ref.at[pl.ds(pl.multiple_of(8 * x, 8), 8)]
+        block = g_ref.at[:, pl.ds(4 * x, 4)]
         to = 8 * lax.rem(own_x + d, 4) + own_y
         return remote(block, block, b_send.at[d], b_recv.at[d], {"lon": to})
 
@@ -113,7 +120,9 @@
         w_go(y_copy(d, lon))
     lax.fori_loop(1, NLON, start_m, 0)
     own_m = pltpu.make_async_copy(m_ref.at[lon], r_ref.at[lon], own_sem.at[1])
-    own_w = pltpu.make_async_copy(wp_ref.at[lat], g_ref.at[lon], own_sem.at[2])
+    own_w = pltpu.make_async_copy(
+        wp_ref.at[lat], g_ref.at[lax.rem(lon, 2), lon // 2], own_sem.at[2]
+    )
     own_m.start()
     own_w.start()
     q = lax.broadcasted_iota(jnp.int32, (64, 256), 0)
@@ -183,7 +192,7 @@
     def take_m(j, c):
         src = lax.rem(lon + NLON - j, NLON)
         remote(
-            m_ref.at[lon], r_ref.at[src], m_send.at[src], m_recv.at[src], {"lon": src}
+            m_ref.at[lon], r_ref.at[src], m_send.at[0], m_recv.at[src], {"lon": src}
         ).wait_recv()
         hand_on(src)
         return c
@@ -240,51 +249,61 @@
     def below(n, start):
         return lax.rem(start + 2 * NLAT - 2 * n, NLAT)
 
+    def exists(at, part):
+        if part == 0:
+            return at < NLAT - 1
+        return (lax.rem(at, 2) == 0) | (at == 11) | (at == 13)
+
     started = []
 
-    def go(copy):
-        copy.start()
-        started.append(copy)
-
-    def part(n, at, half):
-        return ga_ref.at[at] if n < 3 else ga_ref.at[at, pl.ds(16 * half, 16)]
-
-    def ring_up(n):
-        dst = part(n, below(n, lat), 0)
-        return remote(g_ref if n == 0 else dst, dst, c_send.at[n], c_recv.at[n], {"lat": up2})
-
-    def ring_down(n):
-        dst = part(n, above(n, lat), 1)
-        return remote(
-            g_ref if n == 0 else dst, dst, c_send.at[4 + n], c_recv.at[4 + n], {"lat": down2}
-        )
-
-    def to_twin(slot, piece, src):
-        return remote(src, ga_ref.at[piece], s_send.at[slot], s_recv.at[slot], {"lat": twin})
+    def go(at, part, make):
+        make().start()
+        started.append((at, part, make))
+
+    def ring(way, n, part):
+        place = ga_ref.at[(below, above)[way](n, lat), part]
+        slot = 8 * way + 2 * n + part
+        to = {"lat": (up2, down2)[way]}
+        return remote(place, place, c_send.at[slot], c_recv.at[slot], to)
+
+    def to_twin(slot, at, part):
+        place = ga_ref.at[at, part]
+        n = 2 * slot + part
+        return remote(place, place, s_send.at[n], s_recv.at[n], {"lat": twin})
 
     def ring_step(n):
-        piece = below(n, lat)
-        came = part(n - 1, piece, 0)
-        remote(came, came, c_send.at[n - 1], c_recv.at[n - 1], {"lat": up2}).wait_recv()
-        if n < 4:
-            go(ring_up(n))
-            go(to_twin(n, piece, ga_ref.at[piece]))
-        other = above(n, lat)
-        came = part(n - 1, other, 1)
-        remote(came, came, c_send.at[3 + n], c_recv.at[3 + n], {"lat": down2}).wait_recv()
-        if n < 4:
-            go(ring_down(n))
-            go(to_twin(4 + n, other, ga_ref.at[other]))
-        else:
-            go(to_twin(n, piece, ga_ref.at[piece]))
+        for way in range(2):
+            for part in range(2):
+                if n == 4 and part != way:
+                    continue
+                at = (below, above)[way](n, lat)
+
+                @pl.when(exists(at, part))
+                def _():
+                    place = ga_ref.at[at, part]
+                    slot = 8 * way + 2 * (n - 1) + part
+                    remote(
+                        place, place, c_send.at[slot], c_recv.at[slot], {"lat": (up2, down2)[way]}
+                    ).wait_recv()
+                    if n < 3 or (n == 3 and part == way):
+                        go(at, part, functools.partial(ring, way, n, part))
+                    spot = n if way == 0 or n == 4 else 4 + n
+                    go(at, part, functools.partial(to_twin, spot, at, part))
 
     for d in range(1, 4):
         x_block(d, lax.rem(own_x + 4 - d, 4)).wait_recv()
-    own_g = pltpu.make_async_copy(g_ref, ga_ref.at[lat], own_sem.at[4])
-    go(ring_up(0))
-    go(ring_down(0))
-    own_g.start()
-    go(to_twin(0, lat, g_ref))
+    whole = exists(lat, 1)
+    even, odds = g_ref[0].astype(F32), g_ref[1]
+    ga_ref[lat, 0] = jnp.where(whole, even, even + odds.astype(F32)).astype(BF16)
+    ga_ref[lat, 1] = odds
+    for part in range(2):
+
+        @pl.when(exists(lat, part))
+        def _():
+            for way in range(2):
+                go(lat, part, functools.partial(ring, way, 0, part))
+            go(lat, part, functools.partial(to_twin, 0, lat, part))
+
 
     k_up.wait_recv()
     k_down.wait_recv()
@@ -331,8 +350,8 @@
                     n = m
             a_ref[8 * x + y] = jnp.concatenate(parts + [tail], axis=1).astype(BF16)
 
-        def start_a(n, c, x=x):
-            send_a(8 * x + lax.rem(own_y + n, 8)).start()
+        def start_a(n, c, x=x, step=step):
+            send_a(8 * x + lax.rem(own_y + n, 8), step).start()
             return c
 
         lax.fori_loop(1 if step == 0 else 0, 8, start_a, 0)
@@ -344,38 +363,36 @@
         ring_step(n)
 
     for slot in range(8):
-        piece = below(slot, twin) if slot < 5 else above(slot - 4, twin)
-        remote(
-            g_ref, ga_ref.at[piece], s_send.at[slot], s_recv.at[slot], {"lat": twin}
-        ).wait_recv()
-    own_g.wait()
-
-    def order(n, c):
-        k, x = n // 4, lax.rem(n, 4)
-        piece = [
-            ga_ref[3 * k + r, pl.ds(pl.multiple_of(8 * x, 8), 8)].astype(F32).reshape(4, 2, 8, 640)
-            for r in range(3)
-        ]
-        even = [v[:, 0] for v in piece]
-        odds = [v[:, 1] for v in piece]
-        w = jnp.stack([even[0], even[1], even[2] + odds[0], odds[1], odds[2]], axis=1)
-        w = jnp.concatenate([w.reshape(160, 640), jnp.zeros((96, 640), F32)], axis=0)
-        wv_ref[x, pl.ds(pl.multiple_of(256 * k, 256), 256)] = w.astype(BF16)
-        return c
-
-    lax.fori_loop(0, 20, order, 0)
+        at = below(slot, twin) if slot < 5 else above(slot - 4, twin)
+        for part in range(2):
+
+            @pl.when(exists(at, part))
+            def _():
+                to_twin(slot, at, part).wait_recv()
+
+    for k in range(5):
+
+        def order(x, c, k=k):
+            def cut(at, part):
+                return ga_ref[at, part, pl.ds(4 * x, 4)].astype(F32)
+
+            one, two = FULL[2 * k], FULL[2 * k + 1]
+            w = jnp.stack(
+                [cut(one, 0), cut(two, 0), cut(2 * k + 1, 0), cut(one, 1), cut(two, 1)], axis=1
+            )
+            w = jnp.concatenate([w.reshape(160, 640), jnp.zeros((96, 640), F32)], axis=0)
+            wv_ref[x, 256 * k : 256 * k + 256] = w.astype(BF16)
+            return c
+
+        lax.fori_loop(0, 4, order, 0)
 
     for step in range(4):
         x = lax.rem(own_x + 4 - step, 4)
 
-        def take_a(n, c, x=x):
-            src = 8 * x + lax.rem(own_y + n, 8)
-            remote(
-                a_ref.at[lon], ra_ref.at[src], a_send.at[src], a_recv.at[src], {"lon": src}
-            ).wait_recv()
-            return c
-
-        lax.fori_loop(1 if step == 0 else 0, 8, take_a, 0)
+        count = pl.ds(0, 7 if step == 0 else 8)
+        remote(
+            a_ref.at[count], ra_ref.at[count], a_send.at[0], a_recv.at[step], {"lon": peer(1)}
+        ).wait_recv()
         if step == 0:
             own_a.wait()
         for e in range(2):
@@ -397,14 +414,17 @@
                 for o in range(4):
                     o_ref[e, o] = v[e, :, o].reshape(24, 640).astype(BF16)
 
-    def finish(j, c):
-        send_a(peer(j)).wait_send()
-        send_m(j).wait_send()
-        return c
-
-    lax.fori_loop(1, NLON, finish, 0)
-    for copy in started + w_started + [k_up, k_down, h_up, h_down]:
+    others = pl.ds(0, NLON - 1)
+    to = {"lon": peer(1)}
+    remote(m_ref.at[others], r_ref.at[others], m_send.at[0], m_recv.at[0], to).wait_send()
+    remote(a_ref.at[others], ra_ref.at[others], a_send.at[0], a_recv.at[0], to).wait_send()
+    for copy in w_started + [k_up, k_down, h_up, h_down]:
         copy.wait_send()
+    for at, part, make in started:
+
+        @pl.when(exists(at, part))
+        def _():
+            make().wait_send()
 
 
 def per_device(fields, kernel, band_low, block_shift, mix_weight):
@@ -428,7 +448,7 @@
             vmem((16, 8, 640), BF16),
             vmem((32, 32, 128), BF16),
             vmem((2, 32, 32, 128), BF16),
-            vmem((32, 8, 640), BF16),
+            vmem((2, 16, 8, 640), BF16),
             vmem((2, 5, 2, 192, 128), BF16),
             vmem((2, 5, 2, 192, 128), BF16),
             vmem((8, 12, 40, 128), F32),
@@ -439,13 +459,13 @@
             vmem((5, 64, 256), BF16),
             vmem((2, 128, 256), BF16),
             vmem((32, 40, 512), BF16),
-            vmem((16, 32, 8, 640), BF16),
+            vmem((16, 2, 16, 8, 640), BF16),
             vmem((4, 1280, 640), BF16),
             vmem((192, 1280), BF16),
             vmem((192, 640), F32),
-            dma((32,)), dma((32,)), dma((8,)), dma((8,)), dma((4,)), dma((4,)),
-            dma((32,)), dma((32,)), dma((2,)), dma((2,)), dma((2,)), dma((2,)),
-            dma((8,)), dma((8,)), dma((8,)), dma((8,)), dma((7,)),
+            dma((1,)), dma((32,)), dma((8,)), dma((8,)), dma((4,)), dma((4,)),
+            dma((1,)), dma((4,)), dma((2,)), dma((2,)), dma((2,)), dma((2,)),
+            dma((16,)), dma((16,)), dma((16,)), dma((16,)), dma((7,)),
         ],
         compiler_params=pltpu.CompilerParams(collective_id=0, has_side_effects=True),
         name="layer",

time: 69 us -> 66.3 us (0.961)
  the two profiles are of different devices: /device:TPU:1 before, /device:TPU:6 now
where the time goes in v4:
time: 66.3 us; the launch traced here: 66.1 us
  Pallas kernels  64.5 us (97%)
  local copies, waits for them, and re-layouts  1.66 us (3%)
    pallas_call x1, Pallas kernels, per_device(): pl.pallas_call(layer_kernel, out_shape=shape((2, 4, 24, 640), BF16), in_s...  64.5 us
    unnamed x1, local copies, waits for them, and re-layouts  1.66 us

profile of v4, /device:TPU:6, one launch (start us, length us, event | category | flops | bytes accessed | tf_op | source)
XLA Modules:
  0.0 66.1 jit_solution(18255835659420197014)
XLA Ops:
  0.0 64.5 %layer.1 = bf16[2,4,24,640]{3,2,1,0:T(8,128)(2,1)} custom-call(s32[5,64]{1,0:T(8,128)} %low_ref.1, s32[3,64]{1,0:T(4,128)} %bitcast.3, bf16[2,4,24,640]{3,2,1,0:T(8,128)(2,1)} %bitcast.2, bf16[5,20,640]{2,1,0:T(8,128)(2,1)} %w_hbm.1, bf16[5,4,3,3,64,64]{5,4,3,2,1,0:T(8,128)(2,1)} %k_hbm.1), custom_call_target="tpu_custom_call" | custom-call | tf_op jit(solution)/shard_map/layer/pallas_call | solution.py:438
  64.5 1.7 %copy.7 = bf16[2,4,24,640]{3,2,1,0:T(8,128)(2,1)} copy(bf16[2,4,24,640]{3,2,1,0:T(8,128)(2,1)} %layer.1) | data formatting | bytes 491520

commit v5 on v4

--- a/solution.py
+++ b/solution.py
@@ -26,8 +26,8 @@
 
 
 def layer_kernel(
-    low_ref, shift_ref, f_hbm, w_hbm, k_hbm, o_ref,
-    f_ref, w_ref, k_ref, m_ref, wp_ref, r_ref, rh_ref, g_ref, ku_ref, kh_ref,
+    low_hbm, shift_hbm, f_hbm, w_hbm, k_hbm, o_ref,
+    low_ref, shift_ref, f_ref, w_ref, k_ref, m_ref, wp_ref, r_ref, rh_ref, g_ref, ku_ref, kh_ref,
     x_ref, lhs_ref, rhs_ref, acc_ref, a_ref, sp_ref, sq_ref,
     ra_ref, ga_ref, wv_ref, t_ref, sum_ref,
     m_send, m_recv, y_send, y_recv, b_send, b_recv, a_send, a_recv,
@@ -44,7 +44,11 @@
     f_copy = pltpu.make_async_copy(f_hbm, f_ref, own_sem.at[5])
     w_copy = pltpu.make_async_copy(w_hbm, w_ref, own_sem.at[6])
     k_copy = pltpu.make_async_copy(k_hbm, k_ref, own_sem.at[0])
+    low_copy = pltpu.make_async_copy(low_hbm, low_ref, own_sem.at[4])
+    shift_copy = pltpu.make_async_copy(shift_hbm, shift_ref, own_sem.at[7])
     f_copy.start()
+    low_copy.start()
+    shift_copy.start()
     w_copy.start()
     k_copy.start()
 
@@ -116,9 +120,9 @@
         to = 8 * lax.rem(own_x + d, 4) + own_y
         return remote(block, block, b_send.at[d], b_recv.at[d], {"lon": to})
 
+    lax.fori_loop(1, NLON, start_m, 0)
     for d in range(1, 8):
         w_go(y_copy(d, lon))
-    lax.fori_loop(1, NLON, start_m, 0)
     own_m = pltpu.make_async_copy(m_ref.at[lon], r_ref.at[lon], own_sem.at[1])
     own_w = pltpu.make_async_copy(
         wp_ref.at[lat], g_ref.at[lax.rem(lon, 2), lon // 2], own_sem.at[2]
@@ -135,6 +139,8 @@
     sp_ref[4] = jnp.zeros((64, 256), BF16)
 
     k_copy.wait()
+    low_copy.wait()
+    shift_copy.wait()
 
     def pack_halo(k, c):
         for side in range(2):
@@ -175,11 +181,6 @@
 
     lax.fori_loop(0, 5, own_rows, 0)
 
-    own_w.wait()
-    for d in range(1, 8):
-        y_copy(d, 8 * own_x + lax.rem(own_y + 8 - d, 8)).wait_recv()
-    for d in range(1, 4):
-        w_go(x_block(d, own_x))
 
     def hand_on(src):
         remote(
@@ -241,6 +242,11 @@
             lax.fori_loop(0, 4, group, 0)
 
     turn(lambda u: r_ref[u : u + 16], 2, (0, 1, 2, 3))
+    own_w.wait()
+    for d in range(1, 8):
+        y_copy(d, 8 * own_x + lax.rem(own_y + 8 - d, 8)).wait_recv()
+    for d in range(1, 4):
+        w_go(x_block(d, own_x))
     gather((2, 3, 4, 5))
 
     def above(n, start):
@@ -290,21 +296,6 @@
                     spot = n if way == 0 or n == 4 else 4 + n
                     go(at, part, functools.partial(to_twin, spot, at, part))
 
-    for d in range(1, 4):
-        x_block(d, lax.rem(own_x + 4 - d, 4)).wait_recv()
-    whole = exists(lat, 1)
-    even, odds = g_ref[0].astype(F32), g_ref[1]
-    ga_ref[lat, 0] = jnp.where(whole, even, even + odds.astype(F32)).astype(BF16)
-    ga_ref[lat, 1] = odds
-    for part in range(2):
-
-        @pl.when(exists(lat, part))
-        def _():
-            for way in range(2):
-                go(lat, part, functools.partial(ring, way, 0, part))
-            go(lat, part, functools.partial(to_twin, 0, lat, part))
-
-
     k_up.wait_recv()
     k_down.wait_recv()
 
@@ -321,6 +312,21 @@
 
     h_up.wait_recv()
     h_down.wait_recv()
+    for d in range(1, 4):
+        x_block(d, lax.rem(own_x + 4 - d, 4)).wait_recv()
+    whole = exists(lat, 1)
+    even, odds = g_ref[0].astype(F32), g_ref[1]
+    ga_ref[lat, 0] = jnp.where(whole, even, even + odds.astype(F32)).astype(BF16)
+    ga_ref[lat, 1] = odds
+    for part in range(2):
+
+        @pl.when(exists(lat, part))
+        def _():
+            for way in range(2):
+                go(lat, part, functools.partial(ring, way, 0, part))
+            go(lat, part, functools.partial(to_twin, 0, lat, part))
+
+
     turn(lambda u: rh_ref[0, u : u + 16], -2, (2, 3))
     turn(lambda u: rh_ref[1, u : u + 16], 6, (0, 1))
     gather((0, 1, 6, 7))
@@ -429,7 +435,6 @@
 
 def per_device(fields, kernel, band_low, block_shift, mix_weight):
     whole = pl.BlockSpec(memory_space=pltpu.VMEM)
-    smem = pl.BlockSpec(memory_space=pltpu.SMEM)
     anywhere = pl.BlockSpec(memory_space=pl.ANY)
     shape = jax.ShapeDtypeStruct
     dma = pltpu.SemaphoreType.DMA
@@ -437,10 +442,12 @@
 
     return pl.pallas_call(
         layer_kernel,
-        out_shape=shape((2, 4, 24, 640), BF16),
-        in_specs=[smem, smem, anywhere, anywhere, anywhere],
+        out_shape=pltpu.VMEM((2, 4, 24, 640), BF16),
+        in_specs=[anywhere] * 5,
         out_specs=whole,
         scratch_shapes=[
+            pltpu.SMEM((5, 64), jnp.int32),
+            pltpu.SMEM((3, 64), jnp.int32),
             vmem((2, 4, 24, 640), BF16),
             vmem((5, 20, 640), BF16),
             vmem((5, 4, 3, 3, 64, 64), BF16),
@@ -465,7 +472,7 @@
             vmem((192, 640), F32),
             dma((1,)), dma((32,)), dma((8,)), dma((8,)), dma((4,)), dma((4,)),
             dma((1,)), dma((4,)), dma((2,)), dma((2,)), dma((2,)), dma((2,)),
-            dma((16,)), dma((16,)), dma((16,)), dma((16,)), dma((7,)),
+            dma((16,)), dma((16,)), dma((16,)), dma((16,)), dma((8,)),
         ],
         compiler_params=pltpu.CompilerParams(collective_id=0, has_side_effects=True),
         name="layer",

time: 66.3 us -> 63.9 us (0.964)
  the two profiles are of different devices: /device:TPU:6 before, /device:TPU:1 now
where the time goes in v5:
time: 63.9 us; the launch traced here: 62.8 us
  Pallas kernels  62.1 us (97%)
  local copies, waits for them, and re-layouts  0.7 us (1%)
    pallas_call x1, Pallas kernels, per_device(): pl.pallas_call(layer_kernel, out_shape=pltpu.VMEM((2, 4, 24, 640), BF16),...  62.1 us

profile of v5, /device:TPU:1, one launch (start us, length us, event | category | flops | bytes accessed | tf_op | source)
XLA Modules:
  0.0 62.8 jit_solution(14130809217115474906)
XLA Ops:
  0.0 62.1 %layer.1 = bf16[2,4,24,640]{3,2,1,0:T(8,128)(2,1)S(1)} custom-call(s32[5,64]{1,0:T(8,128)} %low_hbm.1, s32[3,64]{1,0:T(4,128)} %bitcast.3, bf16[2,4,24,640]{3,2,1,0:T(8,128)(2,1)} %bitcast.2, bf16[5,20,640]{2,1,0:T(8,128)(2,1)} %w_hbm.1, bf16[5,4,3,3,64,64]{5,4,3,2,1,0:T(8,128)(2,1)} %k_hbm.1), custom_call_target="tpu_custom_call" | custom-call | tf_op jit(solution)/shard_map/layer/pallas_call | solution.py:443
  62.1 0.7 %copy.7 = bf16[2,4,24,640]{3,2,1,0:T(8,128)(2,1)} copy(bf16[2,4,24,640]{3,2,1,0:T(8,128)(2,1)S(1)} %layer.1) | data formatting | bytes 491520

commit v6 on v5

--- a/solution.py
+++ b/solution.py
@@ -28,8 +28,8 @@
 def layer_kernel(
     low_hbm, shift_hbm, f_hbm, w_hbm, k_hbm, o_ref,
     low_ref, shift_ref, f_ref, w_ref, k_ref, m_ref, wp_ref, r_ref, rh_ref, g_ref, ku_ref, kh_ref,
-    x_ref, lhs_ref, rhs_ref, acc_ref, a_ref, sp_ref, sq_ref,
-    ra_ref, ga_ref, wv_ref, t_ref, sum_ref,
+    x_ref, lhs_ref, rhs_ref, acc_ref, a_ref, b_ref, sp_ref, sq_ref,
+    ra_ref, rb_ref, ga_ref, wv_ref, t_ref, sum_ref,
     m_send, m_recv, y_send, y_recv, b_send, b_recv, a_send, a_recv,
     h_send, h_recv, k_send, k_recv, c_send, c_recv, s_send, s_recv, own_sem,
 ):
@@ -99,6 +99,11 @@
     def send_a(to, step):
         return remote(a_ref.at[to], ra_ref.at[lon], a_send.at[0], a_recv.at[step], {"lon": to})
 
+    def send_b(to, step):
+        return remote(
+            b_ref.at[to], rb_ref.at[lon], a_send.at[1], a_recv.at[4 + step], {"lon": to}
+        )
+
     def start_m(j, c):
         send_m(j).start()
         return c
@@ -330,8 +335,9 @@
     turn(lambda u: rh_ref[0, u : u + 16], -2, (2, 3))
     turn(lambda u: rh_ref[1, u : u + 16], 6, (0, 1))
     gather((0, 1, 6, 7))
-    tail = jnp.zeros((40, 32), F32)
+    tail = jnp.zeros((8, 32), F32)
     own_a = pltpu.make_async_copy(a_ref.at[lon], ra_ref.at[lon], own_sem.at[3])
+    own_b = pltpu.make_async_copy(b_ref.at[lon], rb_ref.at[lon], own_sem.at[8])
     for step in range(4):
         x = lax.rem(own_x + step, 4)
 
@@ -354,15 +360,23 @@
                         acc_ref[k, 40 * beta : 40 * beta + 40, 32 * qg : 32 * (qg + m - n)]
                     )
                     n = m
-            a_ref[8 * x + y] = jnp.concatenate(parts + [tail], axis=1).astype(BF16)
+            value = jnp.concatenate(parts, axis=1)
+            a_ref[8 * x + y] = value[:, 0:384].astype(BF16)
+            last = value[:, 384:480]
+            side = [last[32:40, 32 * n : 32 * n + 32] for n in range(3)]
+            side = jnp.concatenate(side + [tail], axis=0)
+            b_ref[8 * x + y] = jnp.concatenate([last[0:32], side], axis=1).astype(BF16)
 
         def start_a(n, c, x=x, step=step):
-            send_a(8 * x + lax.rem(own_y + n, 8), step).start()
+            to = 8 * x + lax.rem(own_y + n, 8)
+            send_a(to, step).start()
+            send_b(to, step).start()
             return c
 
         lax.fori_loop(1 if step == 0 else 0, 8, start_a, 0)
         if step == 0:
             own_a.start()
+            own_b.start()
         elif step == 1:
             ring_step(1)
     for n in range(2, 5):
@@ -399,10 +413,20 @@
         remote(
             a_ref.at[count], ra_ref.at[count], a_send.at[0], a_recv.at[step], {"lon": peer(1)}
         ).wait_recv()
+        remote(
+            b_ref.at[count], rb_ref.at[count], a_send.at[1], a_recv.at[4 + step], {"lon": peer(1)}
+        ).wait_recv()
         if step == 0:
             own_a.wait()
+            own_b.wait()
         for e in range(2):
-            parts = [ra_ref[8 * x + 2 * g + e].astype(F32) for g in range(4)]
+            parts = []
+            for g in range(4):
+                last = rb_ref[8 * x + 2 * g + e].astype(F32)
+                side = [last[8 * n : 8 * n + 8, 96:128] for n in range(3)]
+                both = [last[:, 0:96], jnp.concatenate(side, axis=1)]
+                wide = [ra_ref[8 * x + 2 * g + e].astype(F32), jnp.concatenate(both, axis=0)]
+                parts.append(jnp.concatenate(wide + [jnp.zeros((40, 32), F32)], axis=1))
             turned = jnp.concatenate(parts + [jnp.zeros((96, 512), F32)], axis=0).T.astype(BF16)
             for k in range(5):
                 t_ref[96 * e : 96 * e + 96, 256 * k : 256 * k + 256] = turned[
@@ -424,6 +448,7 @@
     to = {"lon": peer(1)}
     remote(m_ref.at[others], r_ref.at[others], m_send.at[0], m_recv.at[0], to).wait_send()
     remote(a_ref.at[others], ra_ref.at[others], a_send.at[0], a_recv.at[0], to).wait_send()
+    remote(b_ref.at[others], rb_ref.at[others], a_send.at[1], a_recv.at[4], to).wait_send()
     for copy in w_started + [k_up, k_down, h_up, h_down]:
         copy.wait_send()
     for at, part, make in started:
@@ -462,17 +487,19 @@
             vmem((4, 120, 2048), BF16),
             vmem((5, 2048, 256), BF16),
             vmem((5, 120, 256), F32),
-            vmem((32, 40, 512), BF16),
+            vmem((32, 40, 384), BF16),
+            vmem((32, 32, 128), BF16),
             vmem((5, 64, 256), BF16),
             vmem((2, 128, 256), BF16),
-            vmem((32, 40, 512), BF16),
+            vmem((32, 40, 384), BF16),
+            vmem((32, 32, 128), BF16),
             vmem((16, 2, 16, 8, 640), BF16),
             vmem((4, 1280, 640), BF16),
             vmem((192, 1280), BF16),
             vmem((192, 640), F32),
             dma((1,)), dma((32,)), dma((8,)), dma((8,)), dma((4,)), dma((4,)),
-            dma((1,)), dma((4,)), dma((2,)), dma((2,)), dma((2,)), dma((2,)),
-            dma((16,)), dma((16,)), dma((16,)), dma((16,)), dma((8,)),
+            dma((2,)), dma((8,)), dma((2,)), dma((2,)), dma((2,)), dma((2,)),
+            dma((16,)), dma((16,)), dma((16,)), dma((16,)), dma((9,)),
         ],
         compiler_params=pltpu.CompilerParams(collective_id=0, has_side_effects=True),
         name="layer",

time: 63.9 us -> 63 us (0.986); the launches traced: 62.8 us -> 62.9 us
  no operation moved by 1% of the time
where the time goes in v6:
time: 63 us; the launch traced here: 62.9 us
  Pallas kernels  62.2 us (99%)
  local copies, waits for them, and re-layouts  0.7 us (1%)
    pallas_call x1, Pallas kernels, per_device(): pl.pallas_call(layer_kernel, out_shape=pltpu.VMEM((2, 4, 24, 640), BF16),...  62.2 us

profile of v6, /device:TPU:1, one launch (start us, length us, event | category | flops | bytes accessed | tf_op | source)
XLA Modules:
  0.0 62.9 jit_solution(10226588553530257265)
XLA Ops:
  0.0 62.2 %layer.1 = bf16[2,4,24,640]{3,2,1,0:T(8,128)(2,1)S(1)} custom-call(s32[5,64]{1,0:T(8,128)} %low_hbm.1, s32[3,64]{1,0:T(4,128)} %bitcast.3, bf16[2,4,24,640]{3,2,1,0:T(8,128)(2,1)} %bitcast.2, bf16[5,20,640]{2,1,0:T(8,128)(2,1)} %w_hbm.1, bf16[5,4,3,3,64,64]{5,4,3,2,1,0:T(8,128)(2,1)} %k_hbm.1), custom_call_target="tpu_custom_call" | custom-call | tf_op jit(solution)/shard_map/layer/pallas_call | solution.py:468
  62.2 0.7 %copy.7 = bf16[2,4,24,640]{3,2,1,0:T(8,128)(2,1)} copy(bf16[2,4,24,640]{3,2,1,0:T(8,128)(2,1)S(1)} %layer.1) | data formatting | bytes 491520
